TPU v7x, 512 devices: a whole 4x8x8 slice. The times are simulated.
512 devices in a mesh: wide: 32 (over y, x), narrow: 16 (over z, core).
Axes of the slice: x: 4, y: 8, z: 8, core: 2. Of those that a mesh axis runs over, the one named last changes fastest.
Arguments:
- pops_in: float32 [2560, 19, 512], P(('wide', 'narrow')), may hold values from 0 to 1, as said below
- keep_slot: int32 [1536], P(('wide', 'narrow')), may hold values from -1 to 4, as said below
- send_slot: int32 [1024], P(('wide', 'narrow')), may hold values from -1 to 4, as said below
- send_dest: int32 [1024], P(('wide', 'narrow')), may hold values from -1 to 47, as said below
- neighbours: int32 [1536, 18], P(('wide', 'narrow')), may hold values from -1 to 143, as said below
- fluid: int32 [1536, 512], P(('wide', 'narrow')), may hold values 0 or 1
Outputs:
- populations: float32 [1536, 19, 512], P(('wide', 'narrow'))
Inputs may be any that keep to these rules, and one draw needn't show every extreme that they name: Every block stays within its wide index. The blocks of one device that stay keep their populations; each slot after migration is filled at most once, by keep_slot or by one leaving block. Half of the devices of each wide index end with 3 blocks and half with one; empty slots get no neighbours. `send_slot`: A quarter of the devices of each wide index send exactly 2 blocks each, the others none; every sent block fills a slot that keep_slot leaves empty. Destinations lie on the same wide index as the sender and differ from it in narrow index; send_dest is -1 exactly where send_slot is. `neighbours`: direction j points along c_(j+1); a neighbour in a direction with first component o - 1 lies on wide index w + o - 1, none lies outside the wide range; the relation is symmetric and consistent with the slots after migration; each wide index holds 32 blocks. `pops_in`: positive populations near an equilibrium of density about one and small velocity.
All inputs are finite; a program needn't handle non-finite values. No bound on the sum of `fluid` on one device may be relied on, other than what follows from the above.
Results may differ from a plain program's by a relative error of at most 0.0003.
Values sent between devices are 32-bit elements; how exact they have to be, the bound alone decides.
No kernel may reach another device: no remote copies, remote signals or barrier semaphores. Data moves between devices by JAX's collectives and lax.ppermute only.
A program may use at most 128 MiB of HBM per device.

v0:
```python
import jax
import jax.numpy as jnp
from jax import lax
from jax.experimental import pallas as pl
from jax.experimental.pallas import tpu as pltpu
from jax.sharding import Mesh, PartitionSpec as P

STEPS = 4
HELD = 3
ROWS = 48
PACK = 56
INTERPRET = False

VELOCITY = [
    (0, 0, 0),
    (1, 0, 0), (-1, 0, 0), (0, 1, 0), (0, -1, 0), (0, 0, 1), (0, 0, -1),
    (1, 1, 0), (-1, -1, 0), (1, -1, 0), (-1, 1, 0),
    (1, 0, 1), (-1, 0, -1), (1, 0, -1), (-1, 0, 1),
    (0, 1, 1), (0, -1, -1), (0, 1, -1), (0, -1, 1),
]
WEIGHTS = [1.0 / 3.0] + [1.0 / 18.0] * 6 + [1.0 / 36.0] * 12
OPPOSITE = [0, 2, 1, 4, 3, 6, 5, 8, 7, 10, 9, 12, 11, 14, 13, 16, 15, 18, 17]
UP = [i for i in range(19) if VELOCITY[i][2] == 1]
DOWN = [i for i in range(19) if VELOCITY[i][2] == -1]
NU_ZERO = 0.1
NU_LIMIT = 0.01
LAMBDA_TIME = 10.0
POWER_INDEX = 0.35
OMEGA_ZERO = 1.0 / (3.0 * NU_ZERO + 0.5)
SHEAR_SCALE = 2.1213203435596424
RATE_SCALE = (LAMBDA_TIME * SHEAR_SCALE * OMEGA_ZERO) ** 2
F32 = jnp.float32
BF16 = jnp.bfloat16


def iota(shape, dim):
    return lax.broadcasted_iota(jnp.int32, shape, dim)


def dot(a, b):
    return jnp.dot(a, b, preferred_element_type=F32)


def split(x):
    high = x.astype(BF16)
    rest = x - high.astype(F32)
    middle = rest.astype(BF16)
    low = (rest - middle.astype(F32)).astype(BF16)
    return high, middle, low


def choose(picks, x):
    n = x.shape[1]
    y = dot(picks, jnp.concatenate(split(x), axis=1))
    return y[:, :n] + y[:, n : 2 * n] + y[:, 2 * n :]


def permute_lanes(x, picks):
    m = x.shape[0]
    y = dot(jnp.concatenate(split(x), axis=0), picks)
    return y[:m] + y[m : 2 * m] + y[2 * m :]


def collide(f, fluid):
    def total(indices):
        out = None
        for i in indices:
            out = f[i] if out is None else out + f[i]
        return out

    rho = total(range(19))
    inverse = 1.0 / rho
    u = []
    for a in range(3):
        plus = total([i for i in range(19) if VELOCITY[i][a] == 1])
        minus = total([i for i in range(19) if VELOCITY[i][a] == -1])
        u.append((plus - minus) * inverse)
    base = 1.0 - 1.5 * (u[0] * u[0] + u[1] * u[1] + u[2] * u[2])
    excess = [f[0] - WEIGHTS[0] * rho * base]
    scaled = {}
    for i in range(1, 19, 2):
        c = VELOCITY[i]
        along = None
        for a in range(3):
            if c[a]:
                term = u[a]
                if along is None:
                    along = term if c[a] > 0 else -term
                else:
                    along = along + term if c[a] > 0 else along - term
        if WEIGHTS[i] not in scaled:
            scaled[WEIGHTS[i]] = WEIGHTS[i] * rho
        even = base + 4.5 * along * along
        odd = 3.0 * along
        excess.append(f[i] - scaled[WEIGHTS[i]] * (even + odd))
        excess.append(f[i + 1] - scaled[WEIGHTS[i]] * (even - odd))
    stress = None
    for a in range(3):
        for b in range(a, 3):
            part = None
            for i in range(1, 19):
                sign = VELOCITY[i][a] * VELOCITY[i][b]
                if sign:
                    if part is None:
                        part = excess[i] if sign > 0 else -excess[i]
                    else:
                        part = part + excess[i] if sign > 0 else part - excess[i]
            square = part * part if a == b else 2.0 * (part * part)
            stress = square if stress is None else stress + square
    grown = 1.0 + RATE_SCALE * stress * inverse * inverse
    thinned = jnp.exp(((POWER_INDEX - 1.0) / 2.0) * jnp.log(grown))
    viscosity = NU_LIMIT + (NU_ZERO - NU_LIMIT) * thinned
    rate = 1.0 / (3.0 * viscosity + 0.5)
    wet = fluid == 1.0
    return [jnp.where(wet, f[i] - rate * excess[i], f[OPPOSITE[i]]) for i in range(19)]


def collide_all(f_ref, fluid_ref, fc_ref):
    for g in range(ROWS // 8):
        rows = slice(8 * g, 8 * g + 8)
        done = collide([f_ref[i, rows, :] for i in range(19)], fluid_ref[rows, :])
        for i in range(19):
            fc_ref[i, rows, :] = done[i]


def planes_to_send(fc_ref, zp_ref):
    z = lax.axis_index("z")
    up = ((z + lax.axis_index("core")) % 2) == 0
    for k in range(5):
        @pl.when(up)
        def _():
            zp_ref[ROWS * k : ROWS * (k + 1), :] = fc_ref[UP[k]]

        @pl.when(jnp.logical_not(up))
        def _():
            zp_ref[ROWS * k : ROWS * (k + 1), :] = fc_ref[DOWN[k]]


def pack_kernel(keep, send, dest, nbr, pops, fluid, out, xa, xb):
    xa[...] = jnp.zeros_like(xa)
    xb[...] = jnp.zeros_like(xb)
    for s in range(5):
        slot = jnp.maximum(keep[s] if s < HELD else send[s - HELD], 0)
        for i in range(19):
            rows = slice(10 * s + i // 2, 10 * s + i // 2 + 1)
            (xb if i % 2 else xa)[rows, :] = pops[slot, i : i + 1, :]
    for t in range(HELD):
        xb[10 * t + 9 : 10 * t + 10, :] = fluid[t : t + 1, :].astype(F32)
    k, n = iota((128, 128), 0), iota((128, 128), 1)
    picks = (n == (k % 8) * 16 + k // 8).astype(F32).astype(BF16)
    tiles = [x[:, 128 * q : 128 * q + 128] for x in (xa, xb) for q in range(4)]
    y = permute_lanes(jnp.concatenate(tiles, axis=0), picks)
    lane, row = iota((PACK, 128), 1), iota((PACK, 128), 0)
    values = [keep[t] for t in range(3)] + [dest[j] for j in range(2)]
    values = list(enumerate(values)) + [
        (10 + 18 * t + j, nbr[t, j]) for t in range(3) for j in range(18)
    ]
    line = iota((8, 128), 1)
    table = jnp.zeros((8, 128), jnp.int32)
    for place, value in values:
        table = jnp.where(line == 64 + place, value, table)
    table = jnp.concatenate([table.astype(F32)] * (PACK // 8), axis=0)
    marked = jnp.logical_and(row == 39, lane >= 64)
    for z in range(8):
        acc = table
        for part in range(8):
            piece = y[PACK * part : PACK * part + PACK]
            shift = (16 * part - 16 * z) % 128
            piece = pltpu.roll(piece, shift, 1) if shift else piece
            keep_mask = lane // 16 == part
            if part >= 4:
                keep_mask = jnp.logical_and(keep_mask, row != 39)
            acc = jnp.where(keep_mask, piece, acc)
        out[z] = jnp.where(jnp.logical_or(marked, lane < 128), acc, 0.0)


def place_kernel(got, st, nb, xp):
    tables = got[pl.ds(39, 16, stride=PACK), :]
    row16 = iota((ROWS, 16), 0)
    lane16 = iota((ROWS, 16), 1)
    m16 = row16 // 3
    whose = (m16 % 2) * 8 + m16 // 2
    picks = (lane16 == whose).astype(F32).astype(BF16)
    mine = dot(picks, tables.astype(BF16))
    lane, row = iota((ROWS, 128), 1), iota((ROWS, 128), 0)
    t = row % 3
    kept = jnp.sum(jnp.where(lane == 64 + t, mine, 0.0), axis=1, keepdims=True)
    eye = iota((16, 16), 0) == iota((16, 16), 1)
    lane_t = iota((16, 128), 1)
    found = jnp.full((ROWS, 1), -4096, jnp.int32)
    for j in range(2):
        column = jnp.sum(jnp.where(lane_t == 67 + j, tables, 0.0), axis=1, keepdims=True)
        diagonal = jnp.where(eye, column, 0.0).astype(BF16)
        targets = dot(jnp.ones((ROWS, 16), BF16), diagonal)
        hit = targets == row16.astype(F32)
        where_from = jnp.where(hit, lane16 * PACK + 30 + 10 * j + 4096, 0)
        found = found + jnp.sum(where_from.astype(F32), axis=1, keepdims=True).astype(jnp.int32)
    row1 = iota((ROWS, 1), 0)
    m1 = row1 // 3
    own = ((m1 % 2) * 8 + m1 // 2) * PACK + (row1 % 3) * 10
    source = jnp.where(kept >= 0.0, own, found)
    wide_lane = iota((ROWS, 16 * PACK), 1)
    matrices = [(wide_lane == source + p).astype(F32) for p in range(10)]
    matrices.append((wide_lane == own + 9).astype(F32))
    full = choose(jnp.concatenate(matrices, axis=0).astype(BF16), got[...])
    there = source >= 0
    middle = jnp.logical_and(lane >= 32, lane < 96)
    for i in range(19):
        value = full[ROWS * (i // 2) : ROWS * (i // 2) + ROWS]
        value = pltpu.roll(value, 32 if i % 2 == 0 else 96, 1)
        st[i] = jnp.where(jnp.logical_and(there, middle), value, WEIGHTS[i])
    st[19] = jnp.where(middle, pltpu.roll(full[10 * ROWS : 11 * ROWS], 96, 1), 0.0)
    codes = jnp.zeros((ROWS, 128), F32)
    for k in range(3):
        codes = jnp.where(t == k, pltpu.roll(mine, (128 - 74 - 18 * k) % 128, 1), codes)
    nb[...] = codes
    to_right = ((lax.axis_index("wide") + lax.axis_index("core")) % 2) == 0
    for q in range(5):
        acc = jnp.zeros((ROWS, 128), F32)
        for k in range(4):
            value = st[4 * q + k]
            half = jnp.where(to_right, pltpu.roll(value, 64, 1), pltpu.roll(value, 96, 1))
            half = pltpu.roll(half, 32 * k, 1) if k else half
            acc = jnp.where(lane // 32 == k, half, acc)
        xp[ROWS * q : ROWS * q + ROWS, :] = acc
    xp[ROWS * 5 : ROWS * 6, :] = codes


def start_kernel(st, nb, xg, fc, fluid, nb3, zp, f):
    w = lax.axis_index("wide")
    lane = iota((ROWS, 128), 1)
    left, right = (w + 1) % 2, w % 2
    for i in range(20):
        rows = slice(ROWS * (i // 4), ROWS * (i // 4) + ROWS)
        from_left = xg[left, 0, rows, :]
        from_right = xg[right, 1, rows, :]
        shift = (128 - 32 * (i % 4)) % 128
        from_left = pltpu.roll(from_left, shift, 1) if shift else from_left
        shift = (224 - 32 * (i % 4)) % 128
        from_right = pltpu.roll(from_right, shift, 1) if shift else from_right
        value = jnp.where(lane < 32, from_left, jnp.where(lane < 96, st[i], from_right))
        if i < 19:
            f[i] = value
        else:
            fluid[...] = value
    nb3[0] = xg[left, 0, ROWS * 5 : ROWS * 6, :]
    nb3[1] = nb[...]
    nb3[2] = xg[right, 1, ROWS * 5 : ROWS * 6, :]
    collide_all(f, fluid, fc)
    planes_to_send(fc, zp)


def stream(fc, zg, nb3, f):
    z = lax.axis_index("z")
    planes = 8
    lane = iota((ROWS, 128), 1)
    column, y = lane // 8, lane % 8
    segment = [column < 4, jnp.logical_and(column >= 4, column < 12), column >= 12]
    row1 = iota((ROWS, 1), 0)
    slots = iota((ROWS, ROWS), 1)
    tables = [nb3[g].astype(jnp.int32) for g in range(3)]
    below, above = (z + 1) % 2, z % 2

    def source_rows(g, d):
        if d == (0, 0, 0):
            return row1
        j = VELOCITY.index(d) - 1
        return tables[g][:, j : j + 1] - (1 + d[0]) * ROWS

    f[0] = fc[0]
    for i in range(1, 19):
        cx, cy, cz = VELOCITY[i]
        if cz == 0:
            x = fc[i]
        elif cz == 1:
            k = UP.index(i)
            x = zg[below, 0, ROWS * k : ROWS * (k + 1), :]
        else:
            k = DOWN.index(i)
            x = zg[above, 1, ROWS * k : ROWS * (k + 1), :]
        shift = (8 * cx + cy) % 128
        moved = pltpu.roll(x, shift, 1) if shift else x
        at_y = None
        if cy:
            at_y = y == (0 if cy > 0 else 7)
            moved = jnp.where(at_y, pltpu.roll(x, (8 * cx - 7 * cy) % 128, 1), moved)
        at_x = {}
        if cx > 0:
            at_x = {1: column == 4, 2: column == 12}
            edge = column == 0
        elif cx < 0:
            at_x = {0: column == 3, 1: column == 11}
            edge = column == 15
        if cz:
            at_z = z == (0 if cz > 0 else planes - 1)
        parts = []
        for bx in (0, 1) if cx else (0,):
            for by in (0, 1) if cy else (0,):
                if not (bx or by or cz):
                    continue
                for g in range(3):
                    if bx and g not in at_x:
                        continue
                    d = (-cx * bx, -cy * by, 0)
                    rows = source_rows(g, d)
                    if cz:
                        rows = jnp.where(at_z, source_rows(g, d[:2] + (-cz,)), rows)
                    mask = at_x[g] if bx else segment[g]
                    if by:
                        mask = jnp.logical_and(mask, at_y)
                    parts.append((mask, rows))
        picks = [(rows == slots).astype(F32) for _, rows in parts]
        taken = choose(jnp.concatenate(picks, axis=0).astype(BF16), moved)
        bounced = fc[OPPOSITE[i]]
        out = moved
        for n, (mask, rows) in enumerate(parts):
            value = jnp.where(rows >= 0, taken[ROWS * n : ROWS * n + ROWS], bounced)
            out = jnp.where(mask, value, out)
        if cx:
            out = jnp.where(edge, bounced, out)
        f[i] = out


def step_kernel(fc, zg, nb3, fluid, fc_out, zp, f):
    stream(fc, zg, nb3, f)
    collide_all(f, fluid, fc_out)
    planes_to_send(fc_out, zp)


def last_kernel(fc, zg, nb3, out, f):
    stream(fc, zg, nb3, f)
    first = lax.axis_index("core") == 0
    lane = iota((ROWS, 128), 1)
    out[:, 24:32, :] = jnp.zeros((8, 8, 128), F32)
    for p in range(10):
        value = pltpu.roll(f[2 * p], 96, 1)
        if p < 9:
            value = jnp.where(lane < 64, value, pltpu.roll(f[2 * p + 1], 32, 1))
        for z in range(8):
            a, b = value[6 * z : 6 * z + 3], value[6 * z + 3 : 6 * z + 6]
            out[z, 3 * p : 3 * p + 3, :] = jnp.where(first, a, b)


def unpack_kernel(got, out, y):
    lane = iota((32, 128), 1)
    k, n = iota((128, 128), 0), iota((128, 128), 1)
    picks = (n == (k % 16) * 8 + k // 16).astype(F32).astype(BF16)
    tiles = []
    for part in range(8):
        acc = None
        for z in range(8):
            shift = (16 * z - 16 * part) % 128
            piece = pltpu.roll(got[z], shift, 1) if shift else got[z]
            acc = piece if acc is None else jnp.where(lane // 16 == z, piece, acc)
        tiles.append(acc)
    y[...] = permute_lanes(jnp.concatenate(tiles, axis=0), picks)
    for part in range(8):
        h, q = part // 4, part % 4
        for i in range(h, 19, 2):
            for t in range(HELD):
                row = 32 * part + 3 * (i // 2) + t
                out[t, i : i + 1, 128 * q : 128 * q + 128] = y[row : row + 1, :]


def call(kernel, outs, scratch, *args, smem=0):
    spaces = [pltpu.SMEM] * smem + [pltpu.VMEM] * (len(args) - smem)
    many = isinstance(outs, list)
    shapes = [jax.ShapeDtypeStruct(s, F32) for s in (outs if many else [outs])]
    specs = [pl.BlockSpec(memory_space=pltpu.VMEM) for _ in shapes]
    return pl.pallas_call(
        kernel,
        out_shape=shapes if many else shapes[0],
        in_specs=[pl.BlockSpec(memory_space=s) for s in spaces],
        out_specs=specs if many else specs[0],
        scratch_shapes=[pltpu.VMEM(s, F32) for s in scratch],
        interpret=INTERPRET,
    )(*args)


def solution(mesh):
    slabs, group = mesh.shape["wide"], mesh.shape["narrow"]
    chips = group // 2
    axes = ("wide", "z", "core")
    fine = Mesh(mesh.devices.reshape(slabs, chips, 2), axes)

    def pairs(count, other, index):
        return [
            [index(a, b, c), index((a + 1) % count, b, c)]
            for c in range(2)
            for a in range(c, count, 2)
            for b in range(other)
        ]

    wide_pairs = pairs(slabs, chips, lambda w, z, c: (w * chips + z) * 2 + c)
    z_pairs = pairs(chips, 1, lambda z, _, c: z * 2 + c)

    def both_sides(x, names, groups):
        y = lax.all_gather(x, names, axis_index_groups=groups)
        return lax.all_gather(y, "core")

    def shards(pops_in, keep_slot, send_slot, send_dest, neighbours, fluid):
        packed = call(
            pack_kernel, (8, PACK, 128), [(PACK, 512), (PACK, 512)],
            keep_slot, send_slot, send_dest, neighbours, pops_in, fluid, smem=4,
        )
        planes = lax.all_to_all(packed, "z", 0, 0, tiled=True)
        got = lax.all_gather(planes, "core").reshape(16 * PACK, 128)
        st, nb, xp = call(place_kernel, [(20, ROWS, 128), (ROWS, 128), (6 * ROWS, 128)], [], got)
        xg = both_sides(xp, axes, wide_pairs)
        state = (19, ROWS, 128)
        sent = (5 * ROWS, 128)
        fc, wet, nb3, zp = call(
            start_kernel, [state, (ROWS, 128), (3, ROWS, 128), sent], [state], st, nb, xg
        )
        for step in range(STEPS - 1):
            zg = both_sides(zp, ("z", "core"), z_pairs)
            fc, zp = call(step_kernel, [state, sent], [state], fc, zg, nb3, wet)
        zg = both_sides(zp, ("z", "core"), z_pairs)
        back = call(last_kernel, (8, 32, 128), [state], fc, zg, nb3)
        home = lax.all_to_all(back, "z", 0, 0, tiled=True)
        return call(unpack_kernel, (HELD, 19, 512), [(256, 128)], home)

    placed = (P(axes, None, None), P(axes), P(axes), P(axes), P(axes, None), P(axes, None))
    return jax.shard_map(
        shards, mesh=fine, in_specs=placed, out_specs=P(axes, None, None), check_vma=False
    )
```

profile of v0, /device:TPU:1, one launch (start us, length us, event | category | flops | bytes accessed | tf_op | source)
XLA Modules:
  0.0 105.5 jit_solution(15597849665749825821)
XLA Ops:
  0.0 2.4 %shard_map.64 = f32[8,56,128]{2,1,0:T(8,128)} custom-call(s32[3]{0:T(128)} %keep.1, s32[2]{0:T(128)} %send.1, s32[2]{0:T(128)} %dest.1, s32[3,18]{1,0:T(4,128)} %nbr.1, f32[5,19,512]{2,1,0:T(8,128)} %pops.1, s32[3,512]{1,0:T(4,128)} %fluid.1), custom_call_target="tpu_custom_call" | custom-call | tf_op jit(solution)/shard_map/pallas_call | solution.py:370
  2.4 20.7 %all_to_all.10 = f32[8,56,128]{2,1,0:T(8,128)S(1)} all-to-all(f32[8,56,128]{2,1,0:T(8,128)} %shard_map.64), channel_id=1, replica_groups=mesh['wide'=32,'z'=8,'core'=2] {'z'}, dimensions={0} | all-to-all | bytes 458752 | tf_op jit(solution)/shard_map/all_to_all | solution.py:406
  23.1 4.2 %all-gather = f32[16,56,128]{2,1,0:T(8,128)} all-gather(f32[8,56,128]{2,1,0:T(8,128)S(1)} %all_to_all.10), channel_id=2, replica_groups=mesh['wide'=32,'z'=8,'core'=2] {'core'}, dimensions={0}, use_global_device_ids=true | all-gather | bytes 688128 | tf_op jit(solution)/shard_map/all_gather | solution.py:407
  27.2 3.2 %shard_map.65 = (f32[20,48,128]{2,1,0:T(8,128)}, f32[48,128]{1,0:T(8,128)}, f32[288,128]{1,0:T(8,128)}) custom-call(f32[896,128]{1,0:T(8,128)} %bitcast.16), custom_call_target="tpu_custom_call" | custom-call | tf_op jit(solution)/shard_map/pallas_call | solution.py:370
  30.4 8.8 %all-gather.1 = f32[576,128]{1,0:T(8,128)S(1)} all-gather(f32[288,128]{1,0:T(8,128)} %get-tuple-element.20), channel_id=3, replica_groups={{0,16},{2,18},{4,20},{6,22},{8,24},{10,26},{12,28},{14,30},{32,48},{34,..., dimensions={0}, use_global_device_ids=true | all-gather | bytes 442368 | tf_op jit(solution)/shard_map/all_gather | solution.py:398
  39.2 2.3 %all-gather.2 = f32[4,288,128]{2,1,0:T(8,128)} all-gather(f32[2,288,128]{2,1,0:T(8,128)S(1)} %bitcast.17), channel_id=4, replica_groups=mesh['wide'=32,'z'=8,'core'=2] {'core'}, dimensions={0}, use_global_device_ids=true | all-gather | bytes 884736 | tf_op jit(solution)/shard_map/all_gather | solution.py:399
  41.6 2.6 %shard_map.66 = (f32[19,48,128]{2,1,0:T(8,128)}, f32[48,128]{1,0:T(8,128)}, f32[3,48,128]{2,1,0:T(8,128)}, f32[240,128]{1,0:T(8,128)}) custom-call(f32[20,48,128]{2,1,0:T(8,128)} %get-tuple-element.18.st, f32[48,128]{1,0:T(8,128)} %get-tuple-element.19.nb, f32[2,2,288,128]{3,2,1,0:T(8,128)} %bitcast.11), custom_call_target="tpu_custom_call" | custom-call | tf_op jit(solution)/shard_map/pallas_call | solution.py:370
  44.2 5.8 %all-gather.3 = f32[480,128]{1,0:T(8,128)S(1)} all-gather(f32[240,128]{1,0:T(8,128)} %get-tuple-element.22), channel_id=5, replica_groups={{0,2},{4,6},{8,10},{12,14},{3,5},{7,9},{11,13},{15,1},{16,18},{20,22},{..., dimensions={0}, use_global_device_ids=true | all-gather | bytes 368640 | tf_op jit(solution)/shard_map/all_gather | solution.py:398
  50.0 2.3 %all-gather.4 = f32[4,240,128]{2,1,0:T(8,128)} all-gather(f32[2,240,128]{2,1,0:T(8,128)S(1)} %bitcast.18), channel_id=6, replica_groups=mesh['wide'=32,'z'=8,'core'=2] {'core'}, dimensions={0}, use_global_device_ids=true | all-gather | bytes 737280 | tf_op jit(solution)/shard_map/all_gather | solution.py:399
  52.3 3.6 %shard_map.67 = (f32[19,48,128]{2,1,0:T(8,128)}, f32[240,128]{1,0:T(8,128)}) custom-call(f32[19,48,128]{2,1,0:T(8,128)} %get-tuple-element.21.fc, f32[2,2,240,128]{3,2,1,0:T(8,128)} %bitcast.14, f32[3,48,128]{2,1,0:T(8,128)} %get-tuple-element.23.nb3, f32[48,128]{1,0:T(8,128)} %get-tuple-element.24.fluid), custom_call_target="tpu_custom_call" | custom-call | tf_op jit(solution)/shard_map/pallas_call | solution.py:370
  55.9 5.8 %all-gather.5 = f32[480,128]{1,0:T(8,128)S(1)} all-gather(f32[240,128]{1,0:T(8,128)} %get-tuple-element.26), channel_id=7, replica_groups={{0,2},{4,6},{8,10},{12,14},{3,5},{7,9},{11,13},{15,1},{16,18},{20,22},{..., dimensions={0}, use_global_device_ids=true | all-gather | bytes 368640 | tf_op jit(solution)/shard_map/all_gather | solution.py:398
  61.7 2.3 %all-gather.6 = f32[4,240,128]{2,1,0:T(8,128)} all-gather(f32[2,240,128]{2,1,0:T(8,128)S(1)} %bitcast.19), channel_id=8, replica_groups=mesh['wide'=32,'z'=8,'core'=2] {'core'}, dimensions={0}, use_global_device_ids=true | all-gather | bytes 737280 | tf_op jit(solution)/shard_map/all_gather | solution.py:399
  64.0 3.6 %shard_map.68 = (f32[19,48,128]{2,1,0:T(8,128)}, f32[240,128]{1,0:T(8,128)}) custom-call(f32[19,48,128]{2,1,0:T(8,128)} %get-tuple-element.25.fc, f32[2,2,240,128]{3,2,1,0:T(8,128)} %bitcast.15, f32[3,48,128]{2,1,0:T(8,128)} %get-tuple-element.23.nb3, f32[48,128]{1,0:T(8,128)} %get-tuple-element.24.fluid), custom_call_target="tpu_custom_call" | custom-call | tf_op jit(solution)/shard_map/pallas_call | solution.py:370
  67.6 5.8 %all-gather.7 = f32[480,128]{1,0:T(8,128)S(1)} all-gather(f32[240,128]{1,0:T(8,128)} %get-tuple-element.28), channel_id=9, replica_groups={{0,2},{4,6},{8,10},{12,14},{3,5},{7,9},{11,13},{15,1},{16,18},{20,22},{..., dimensions={0}, use_global_device_ids=true | all-gather | bytes 368640 | tf_op jit(solution)/shard_map/all_gather | solution.py:398
  73.4 2.3 %all-gather.8 = f32[4,240,128]{2,1,0:T(8,128)} all-gather(f32[2,240,128]{2,1,0:T(8,128)S(1)} %bitcast.20), channel_id=10, replica_groups=mesh['wide'=32,'z'=8,'core'=2] {'core'}, dimensions={0}, use_global_device_ids=true | all-gather | bytes 737280 | tf_op jit(solution)/shard_map/all_gather | solution.py:399
  75.6 3.6 %shard_map.69 = (f32[19,48,128]{2,1,0:T(8,128)}, f32[240,128]{1,0:T(8,128)}) custom-call(f32[19,48,128]{2,1,0:T(8,128)} %get-tuple-element.27.fc, f32[2,2,240,128]{3,2,1,0:T(8,128)} %bitcast.13, f32[3,48,128]{2,1,0:T(8,128)} %get-tuple-element.23.nb3, f32[48,128]{1,0:T(8,128)} %get-tuple-element.24.fluid), custom_call_target="tpu_custom_call" | custom-call | tf_op jit(solution)/shard_map/pallas_call | solution.py:370
  79.2 5.8 %all-gather.9 = f32[480,128]{1,0:T(8,128)S(1)} all-gather(f32[240,128]{1,0:T(8,128)} %get-tuple-element.30), channel_id=11, replica_groups={{0,2},{4,6},{8,10},{12,14},{3,5},{7,9},{11,13},{15,1},{16,18},{20,22},{..., dimensions={0}, use_global_device_ids=true | all-gather | bytes 368640 | tf_op jit(solution)/shard_map/all_gather | solution.py:398
  85.1 2.3 %all-gather.10 = f32[4,240,128]{2,1,0:T(8,128)} all-gather(f32[2,240,128]{2,1,0:T(8,128)S(1)} %bitcast.21), channel_id=12, replica_groups=mesh['wide'=32,'z'=8,'core'=2] {'core'}, dimensions={0}, use_global_device_ids=true | all-gather | bytes 737280 | tf_op jit(solution)/shard_map/all_gather | solution.py:399
  87.3 3.4 %shard_map.70 = f32[8,32,128]{2,1,0:T(8,128)} custom-call(f32[19,48,128]{2,1,0:T(8,128)} %get-tuple-element.29.fc, f32[2,2,240,128]{3,2,1,0:T(8,128)} %bitcast.12, f32[3,48,128]{2,1,0:T(8,128)} %get-tuple-element.23.nb3), custom_call_target="tpu_custom_call" | custom-call | tf_op jit(solution)/shard_map/pallas_call | solution.py:370
  90.7 12.7 %all_to_all.11.got = f32[8,32,128]{2,1,0:T(8,128)} all-to-all(f32[8,32,128]{2,1,0:T(8,128)} %shard_map.70), channel_id=1, replica_groups=mesh['wide'=32,'z'=8,'core'=2] {'z'}, dimensions={0} | all-to-all | bytes 262144 | tf_op jit(solution)/shard_map/all_to_all | solution.py:420
  103.4 2.1 %shard_map.71 = f32[3,19,512]{2,1,0:T(8,128)} custom-call(f32[8,32,128]{2,1,0:T(8,128)} %all_to_all.11.got), custom_call_target="tpu_custom_call" | custom-call | tf_op jit(solution)/shard_map/pallas_call | solution.py:370
where the time goes:
time: 106 us
  blocking collectives  81.1 us (77%)
  Pallas kernels  24.4 us (23%)
    all_gather x5, blocking collectives, both_sides(): y = lax.all_gather(x, names, axis_index_groups=groups)  32 us
    pallas_call x8, Pallas kernels, call(): pl.pallas_call(kernel, out_shape=shapes if many else shapes[0], in_specs=...  24.4 us
    all_to_all x1, blocking collectives, shards(): planes = lax.all_to_all(packed, 'z', 0, 0, tiled=True)  20.7 us
    all_to_all x1, blocking collectives, shards(): home = lax.all_to_all(back, 'z', 0, 0, tiled=True)  12.7 us
    all_gather x5, blocking collectives, both_sides(): return lax.all_gather(y, 'core')  11.5 us
    all_gather x1, blocking collectives, shards(): got = lax.all_gather(planes, 'core').reshape(16 * PACK, 128)  4.18 us

commit v1 on v0

--- a/solution.py
+++ b/solution.py
@@ -362,7 +362,7 @@
                 out[t, i : i + 1, 128 * q : 128 * q + 128] = y[row : row + 1, :]
 
 
-def call(kernel, outs, scratch, *args, smem=0):
+def call(kernel, outs, scratch, *args, smem=0, limit=8 * 1024 * 1024):
     spaces = [pltpu.SMEM] * smem + [pltpu.VMEM] * (len(args) - smem)
     many = isinstance(outs, list)
     shapes = [jax.ShapeDtypeStruct(s, F32) for s in (outs if many else [outs])]
@@ -373,6 +373,7 @@
         in_specs=[pl.BlockSpec(memory_space=s) for s in spaces],
         out_specs=specs if many else specs[0],
         scratch_shapes=[pltpu.VMEM(s, F32) for s in scratch],
+        compiler_params=pltpu.CompilerParams(vmem_limit_bytes=limit),
         interpret=INTERPRET,
     )(*args)
 
@@ -402,6 +403,7 @@
         packed = call(
             pack_kernel, (8, PACK, 128), [(PACK, 512), (PACK, 512)],
             keep_slot, send_slot, send_dest, neighbours, pops_in, fluid, smem=4,
+            limit=None,
         )
         planes = lax.all_to_all(packed, "z", 0, 0, tiled=True)
         got = lax.all_gather(planes, "core").reshape(16 * PACK, 128)

time: 106 us -> 90 us (0.85)
  Pallas kernels: 24.4 us -> 12 us
  blocking collectives: 81.1 us -> 77.6 us
    pallas_call x8, Pallas kernels: 24.4 us -> 12 us  [call(): pl.pallas_call(kernel, out_shape=shapes if many else shapes[0], in_specs=...]
    all_to_all x1, blocking collectives: 12.7 us -> 11.1 us  [shards(): home = lax.all_to_all(back, 'z', 0, 0, tiled=True)]
    all_gather x5, blocking collectives: 32 us -> 31 us  [both_sides(): y = lax.all_gather(x, names, axis_index_groups=groups)]
where the time goes in v1:
time: 90 us; the launch traced here: 89.6 us
  blocking collectives  77.6 us (86%)
  Pallas kernels  12 us (13%)
    all_gather x5, blocking collectives, both_sides(): y = lax.all_gather(x, names, axis_index_groups=groups)  31 us
    all_to_all x1, blocking collectives, shards(): planes = lax.all_to_all(packed, 'z', 0, 0, tiled=True)  20.7 us
    pallas_call x8, Pallas kernels, call(): pl.pallas_call(kernel, out_shape=shapes if many else shapes[0], in_specs=...  12 us
    all_to_all x1, blocking collectives, shards(): home = lax.all_to_all(back, 'z', 0, 0, tiled=True)  11.1 us
    all_gather x5, blocking collectives, both_sides(): return lax.all_gather(y, 'core')  10.8 us
    all_gather x1, blocking collectives, shards(): got = lax.all_gather(planes, 'core').reshape(16 * PACK, 128)  4.05 us

profile of v1, /device:TPU:1, one launch (start us, length us, event | category | flops | bytes accessed | tf_op | source)
XLA Modules:
  0.0 89.6 jit_solution(17267604045994674859)
XLA Ops:
  0.0 2.4 %shard_map.64 = f32[8,56,128]{2,1,0:T(8,128)} custom-call(s32[3]{0:T(128)} %keep.1, s32[2]{0:T(128)} %send.1, s32[2]{0:T(128)} %dest.1, s32[3,18]{1,0:T(4,128)} %nbr.1, f32[5,19,512]{2,1,0:T(8,128)} %pops.1, s32[3,512]{1,0:T(4,128)} %fluid.1), custom_call_target="tpu_custom_call" | custom-call | tf_op jit(solution)/shard_map/pallas_call | solution.py:370
  2.4 20.7 %all_to_all.10 = f32[8,56,128]{2,1,0:T(8,128)S(1)} all-to-all(f32[8,56,128]{2,1,0:T(8,128)} %shard_map.64), channel_id=1, replica_groups=mesh['wide'=32,'z'=8,'core'=2] {'z'}, dimensions={0} | all-to-all | bytes 458752 | tf_op jit(solution)/shard_map/all_to_all | solution.py:408
  23.1 4.1 %all-gather = f32[16,56,128]{2,1,0:T(8,128)S(1)} all-gather(f32[8,56,128]{2,1,0:T(8,128)S(1)} %all_to_all.10), channel_id=2, replica_groups=mesh['wide'=32,'z'=8,'core'=2] {'core'}, dimensions={0}, use_global_device_ids=true | all-gather | bytes 688128 | tf_op jit(solution)/shard_map/all_gather | solution.py:409
  27.1 1.4 %shard_map.65 = (f32[20,48,128]{2,1,0:T(8,128)S(1)}, f32[48,128]{1,0:T(8,128)S(1)}, f32[288,128]{1,0:T(8,128)S(1)}) custom-call(f32[896,128]{1,0:T(8,128)S(1)} %bitcast.16), custom_call_target="tpu_custom_call" | custom-call | tf_op jit(solution)/shard_map/pallas_call | solution.py:370
  28.5 8.6 %all-gather.1 = f32[576,128]{1,0:T(8,128)S(1)} all-gather(f32[288,128]{1,0:T(8,128)S(1)} %get-tuple-element.20), channel_id=3, replica_groups={{0,16},{2,18},{4,20},{6,22},{8,24},{10,26},{12,28},{14,30},{32,48},{34,..., dimensions={0}, use_global_device_ids=true | all-gather | bytes 442368 | tf_op jit(solution)/shard_map/all_gather | solution.py:399
  37.1 2.2 %all-gather.2 = f32[4,288,128]{2,1,0:T(8,128)S(1)} all-gather(f32[2,288,128]{2,1,0:T(8,128)S(1)} %bitcast.17), channel_id=4, replica_groups=mesh['wide'=32,'z'=8,'core'=2] {'core'}, dimensions={0}, use_global_device_ids=true | all-gather | bytes 884736 | tf_op jit(solution)/shard_map/all_gather | solution.py:400
  39.3 0.5 shard_map.66
  39.9 5.6 %all-gather.3 = f32[480,128]{1,0:T(8,128)S(1)} all-gather(f32[240,128]{1,0:T(8,128)S(1)} %get-tuple-element.22), channel_id=5, replica_groups={{0,2},{4,6},{8,10},{12,14},{3,5},{7,9},{11,13},{15,1},{16,18},{20,22},{..., dimensions={0}, use_global_device_ids=true | all-gather | bytes 368640 | tf_op jit(solution)/shard_map/all_gather | solution.py:399
  45.5 2.1 %all-gather.4 = f32[4,240,128]{2,1,0:T(8,128)S(1)} all-gather(f32[2,240,128]{2,1,0:T(8,128)S(1)} %bitcast.18), channel_id=6, replica_groups=mesh['wide'=32,'z'=8,'core'=2] {'core'}, dimensions={0}, use_global_device_ids=true | all-gather | bytes 737280 | tf_op jit(solution)/shard_map/all_gather | solution.py:400
  47.6 1.6 %shard_map.67 = (f32[19,48,128]{2,1,0:T(8,128)S(1)}, f32[240,128]{1,0:T(8,128)S(1)}) custom-call(f32[19,48,128]{2,1,0:T(8,128)S(1)} %get-tuple-element.21.fc, f32[2,2,240,128]{3,2,1,0:T(8,128)S(1)} %bitcast.14, f32[3,48,128]{2,1,0:T(8,128)S(1)} %get-tuple-element.23.nb3, f32[48,128]{1,0:T(8,128)S(1)} %get-tuple-element.24.fluid), custom_call_target="tpu_custom_call" | custom-call | tf_op jit(solution)/shard_map/pallas_call | solution.py:370
  49.2 5.6 %all-gather.5 = f32[480,128]{1,0:T(8,128)S(1)} all-gather(f32[240,128]{1,0:T(8,128)S(1)} %get-tuple-element.26), channel_id=7, replica_groups={{0,2},{4,6},{8,10},{12,14},{3,5},{7,9},{11,13},{15,1},{16,18},{20,22},{..., dimensions={0}, use_global_device_ids=true | all-gather | bytes 368640 | tf_op jit(solution)/shard_map/all_gather | solution.py:399
  54.8 2.1 %all-gather.6 = f32[4,240,128]{2,1,0:T(8,128)S(1)} all-gather(f32[2,240,128]{2,1,0:T(8,128)S(1)} %bitcast.19), channel_id=8, replica_groups=mesh['wide'=32,'z'=8,'core'=2] {'core'}, dimensions={0}, use_global_device_ids=true | all-gather | bytes 737280 | tf_op jit(solution)/shard_map/all_gather | solution.py:400
  57.0 1.6 %shard_map.68 = (f32[19,48,128]{2,1,0:T(8,128)S(1)}, f32[240,128]{1,0:T(8,128)S(1)}) custom-call(f32[19,48,128]{2,1,0:T(8,128)S(1)} %get-tuple-element.25.fc, f32[2,2,240,128]{3,2,1,0:T(8,128)S(1)} %bitcast.15, f32[3,48,128]{2,1,0:T(8,128)S(1)} %get-tuple-element.23.nb3, f32[48,128]{1,0:T(8,128)S(1)} %get-tuple-element.24.fluid), custom_call_target="tpu_custom_call" | custom-call | tf_op jit(solution)/shard_map/pallas_call | solution.py:370
  58.6 5.6 %all-gather.7 = f32[480,128]{1,0:T(8,128)S(1)} all-gather(f32[240,128]{1,0:T(8,128)S(1)} %get-tuple-element.28), channel_id=9, replica_groups={{0,2},{4,6},{8,10},{12,14},{3,5},{7,9},{11,13},{15,1},{16,18},{20,22},{..., dimensions={0}, use_global_device_ids=true | all-gather | bytes 368640 | tf_op jit(solution)/shard_map/all_gather | solution.py:399
  64.2 2.1 %all-gather.8 = f32[4,240,128]{2,1,0:T(8,128)S(1)} all-gather(f32[2,240,128]{2,1,0:T(8,128)S(1)} %bitcast.20), channel_id=10, replica_groups=mesh['wide'=32,'z'=8,'core'=2] {'core'}, dimensions={0}, use_global_device_ids=true | all-gather | bytes 737280 | tf_op jit(solution)/shard_map/all_gather | solution.py:400
  66.4 1.7 %shard_map.69 = (f32[19,48,128]{2,1,0:T(8,128)S(1)}, f32[240,128]{1,0:T(8,128)S(1)}) custom-call(f32[19,48,128]{2,1,0:T(8,128)S(1)} %get-tuple-element.27.fc, f32[2,2,240,128]{3,2,1,0:T(8,128)S(1)} %bitcast.13, f32[3,48,128]{2,1,0:T(8,128)S(1)} %get-tuple-element.23.nb3, f32[48,128]{1,0:T(8,128)S(1)} %get-tuple-element.24.fluid), custom_call_target="tpu_custom_call" | custom-call | tf_op jit(solution)/shard_map/pallas_call | solution.py:370
  68.0 5.6 %all-gather.9 = f32[480,128]{1,0:T(8,128)S(1)} all-gather(f32[240,128]{1,0:T(8,128)S(1)} %get-tuple-element.30), channel_id=11, replica_groups={{0,2},{4,6},{8,10},{12,14},{3,5},{7,9},{11,13},{15,1},{16,18},{20,22},{..., dimensions={0}, use_global_device_ids=true | all-gather | bytes 368640 | tf_op jit(solution)/shard_map/all_gather | solution.py:399
  73.7 2.1 %all-gather.10 = f32[4,240,128]{2,1,0:T(8,128)S(1)} all-gather(f32[2,240,128]{2,1,0:T(8,128)S(1)} %bitcast.21), channel_id=12, replica_groups=mesh['wide'=32,'z'=8,'core'=2] {'core'}, dimensions={0}, use_global_device_ids=true | all-gather | bytes 737280 | tf_op jit(solution)/shard_map/all_gather | solution.py:400
  75.8 1.6 %shard_map.70 = f32[8,32,128]{2,1,0:T(8,128)S(1)} custom-call(f32[19,48,128]{2,1,0:T(8,128)S(1)} %get-tuple-element.29.fc, f32[2,2,240,128]{3,2,1,0:T(8,128)S(1)} %bitcast.12, f32[3,48,128]{2,1,0:T(8,128)S(1)} %get-tuple-element.23.nb3), custom_call_target="tpu_custom_call" | custom-call | tf_op jit(solution)/shard_map/pallas_call | solution.py:370
  77.4 11.1 %all_to_all.11.got = f32[8,32,128]{2,1,0:T(8,128)S(1)} all-to-all(f32[8,32,128]{2,1,0:T(8,128)S(1)} %shard_map.70), channel_id=1, replica_groups=mesh['wide'=32,'z'=8,'core'=2] {'z'}, dimensions={0} | all-to-all | bytes 262144 | tf_op jit(solution)/shard_map/all_to_all | solution.py:422
  88.4 1.2 %shard_map.71 = f32[3,19,512]{2,1,0:T(8,128)} custom-call(f32[8,32,128]{2,1,0:T(8,128)S(1)} %all_to_all.11.got), custom_call_target="tpu_custom_call" | custom-call | tf_op jit(solution)/shard_map/pallas_call | solution.py:370

commit v2 on v1

--- a/solution.py
+++ b/solution.py
@@ -9,6 +9,7 @@
 HELD = 3
 ROWS = 48
 PACK = 56
+PLANES = 8
 INTERPRET = False
 
 VELOCITY = [
@@ -21,6 +22,7 @@
 WEIGHTS = [1.0 / 3.0] + [1.0 / 18.0] * 6 + [1.0 / 36.0] * 12
 OPPOSITE = [0, 2, 1, 4, 3, 6, 5, 8, 7, 10, 9, 12, 11, 14, 13, 16, 15, 18, 17]
 UP = [i for i in range(19) if VELOCITY[i][2] == 1]
+FLAT = [i for i in range(19) if VELOCITY[i][2] == 0]
 DOWN = [i for i in range(19) if VELOCITY[i][2] == -1]
 NU_ZERO = 0.1
 NU_LIMIT = 0.01
@@ -250,16 +252,13 @@
     planes_to_send(fc, zp)
 
 
-def stream(fc, zg, nb3, f):
-    z = lax.axis_index("z")
-    planes = 8
+def passing(fc, nb3, segments):
     lane = iota((ROWS, 128), 1)
     column, y = lane // 8, lane % 8
     segment = [column < 4, jnp.logical_and(column >= 4, column < 12), column >= 12]
     row1 = iota((ROWS, 1), 0)
     slots = iota((ROWS, ROWS), 1)
-    tables = [nb3[g].astype(jnp.int32) for g in range(3)]
-    below, above = (z + 1) % 2, z % 2
+    tables = {g: nb3[g].astype(jnp.int32) for g in segments}
 
     def source_rows(g, d):
         if d == (0, 0, 0):
@@ -267,17 +266,8 @@
         j = VELOCITY.index(d) - 1
         return tables[g][:, j : j + 1] - (1 + d[0]) * ROWS
 
-    f[0] = fc[0]
-    for i in range(1, 19):
+    def move(i, x, at_z):
         cx, cy, cz = VELOCITY[i]
-        if cz == 0:
-            x = fc[i]
-        elif cz == 1:
-            k = UP.index(i)
-            x = zg[below, 0, ROWS * k : ROWS * (k + 1), :]
-        else:
-            k = DOWN.index(i)
-            x = zg[above, 1, ROWS * k : ROWS * (k + 1), :]
         shift = (8 * cx + cy) % 128
         moved = pltpu.roll(x, shift, 1) if shift else x
         at_y = None
@@ -291,14 +281,12 @@
         elif cx < 0:
             at_x = {0: column == 3, 1: column == 11}
             edge = column == 15
-        if cz:
-            at_z = z == (0 if cz > 0 else planes - 1)
         parts = []
         for bx in (0, 1) if cx else (0,):
             for by in (0, 1) if cy else (0,):
                 if not (bx or by or cz):
                     continue
-                for g in range(3):
+                for g in segments:
                     if bx and g not in at_x:
                         continue
                     d = (-cx * bx, -cy * by, 0)
@@ -309,6 +297,8 @@
                     if by:
                         mask = jnp.logical_and(mask, at_y)
                     parts.append((mask, rows))
+        if not parts:
+            return moved
         picks = [(rows == slots).astype(F32) for _, rows in parts]
         taken = choose(jnp.concatenate(picks, axis=0).astype(BF16), moved)
         bounced = fc[OPPOSITE[i]]
@@ -318,7 +308,24 @@
             out = jnp.where(mask, value, out)
         if cx:
             out = jnp.where(edge, bounced, out)
-        f[i] = out
+        return out
+
+    return move
+
+
+def stream(fc, zg, nb3, f):
+    z = lax.axis_index("z")
+    below, above = (z + 1) % 2, z % 2
+    move = passing(fc, nb3, (0, 1, 2))
+    for i in range(19):
+        if i in UP:
+            k = UP.index(i)
+            f[i] = move(i, zg[below, 0, ROWS * k : ROWS * (k + 1), :], z == 0)
+        elif i in DOWN:
+            k = DOWN.index(i)
+            f[i] = move(i, zg[above, 1, ROWS * k : ROWS * (k + 1), :], z == PLANES - 1)
+        else:
+            f[i] = move(i, fc[i], None)
 
 
 def step_kernel(fc, zg, nb3, fluid, fc_out, zp, f):
@@ -327,39 +334,84 @@
     planes_to_send(fc_out, zp)
 
 
-def last_kernel(fc, zg, nb3, out, f):
-    stream(fc, zg, nb3, f)
+def last_kernel(fc, nb3, out):
+    z = lax.axis_index("z")
     first = lax.axis_index("core") == 0
     lane = iota((ROWS, 128), 1)
-    out[:, 24:32, :] = jnp.zeros((8, 8, 128), F32)
-    for p in range(10):
-        value = pltpu.roll(f[2 * p], 96, 1)
-        if p < 9:
-            value = jnp.where(lane < 64, value, pltpu.roll(f[2 * p + 1], 32, 1))
-        for z in range(8):
-            a, b = value[6 * z : 6 * z + 3], value[6 * z + 3 : 6 * z + 6]
-            out[z, 3 * p : 3 * p + 3, :] = jnp.where(first, a, b)
-
-
-def unpack_kernel(got, out, y):
-    lane = iota((32, 128), 1)
+    move = passing(fc, nb3, (1,))
+    left = [move(i, fc[i], None) for i in FLAT]
+    left += [move(i, fc[i], z == PLANES - 1) for i in UP] + [None]
+    right = [move(i, fc[i], z == 0) for i in DOWN]
+    right += [fc[OPPOSITE[i]] for i in UP + DOWN]
+    out[:, 40:48, :] = jnp.zeros((PLANES, 8, 128), F32)
+    for p in range(15):
+        value = pltpu.roll(right[p], 32, 1)
+        if left[p] is not None:
+            value = jnp.where(lane < 64, pltpu.roll(left[p], 96, 1), value)
+        for n in range(PLANES):
+            a, b = value[6 * n : 6 * n + 3], value[6 * n + 3 : 6 * n + 6]
+            out[n, 3 * p : 3 * p + 3, :] = jnp.where(first, a, b)
+
+
+def unpack_kernel(got, nbr, out, x):
+    lane, row = iota((48, 128), 1), iota((48, 128), 0)
     k, n = iota((128, 128), 0), iota((128, 128), 1)
     picks = (n == (k % 16) * 8 + k // 16).astype(F32).astype(BF16)
-    tiles = []
-    for part in range(8):
+    place = iota((HELD, 128), 1)
+    here_z, here_y = place // 16, place % 8
+    absent = [nbr[:, j : j + 1] < 0 for j in range(18)]
+    x[...] = jnp.zeros_like(x)
+
+    def gathered(part):
         acc = None
-        for z in range(8):
+        for z in range(PLANES):
             shift = (16 * z - 16 * part) % 128
             piece = pltpu.roll(got[z], shift, 1) if shift else got[z]
             acc = piece if acc is None else jnp.where(lane // 16 == z, piece, acc)
-        tiles.append(acc)
-    y[...] = permute_lanes(jnp.concatenate(tiles, axis=0), picks)
-    for part in range(8):
-        h, q = part // 4, part % 4
-        for i in range(h, 19, 2):
+        return acc
+
+    for q in range(4):
+        a, b = gathered(q), gathered(4 + q)
+        a = jnp.where(row >= 27, pltpu.roll(a, 16, 1), a)
+        b = jnp.where(row < 15, pltpu.roll(b, 112, 1), b)
+        here_x = 2 * q + (place % 16) // 8
+
+        def missing(c):
+            spots = []
+            for size, here, top in zip(c, (here_x, here_y, here_z), (7, 7, 7)):
+                spots.append(None if not size else here == (0 if size > 0 else top))
+            found = jnp.zeros((HELD, 128), jnp.bool_)
+            for flags in range(1, 8):
+                across = [(flags >> s) & 1 for s in range(3)]
+                if any(g and spot is None for g, spot in zip(across, spots)):
+                    continue
+                d = tuple(-size * g for size, g in zip(c, across))
+                mask = jnp.broadcast_to(absent[VELOCITY.index(d) - 1], (HELD, 128))
+                for g, spot in zip(across, spots):
+                    if spot is not None:
+                        mask = jnp.logical_and(mask, spot if g else jnp.logical_not(spot))
+                found = jnp.logical_or(found, mask)
+            return found
+
+        for i in range(19):
+            if i in UP:
+                j = 3 * UP.index(i)
+                bare = b[15 + j : 18 + j]
+                value = jnp.where(missing(VELOCITY[i]), bare, a[27 + j : 30 + j])
+            elif i in DOWN:
+                j = 3 * DOWN.index(i)
+                bare = b[30 + j : 33 + j]
+                value = jnp.where(missing(VELOCITY[i]), bare, b[j : j + 3])
+            else:
+                j = 3 * FLAT.index(i)
+                value = a[j : j + 3]
+            x[64 * q + 3 * i : 64 * q + 3 * i + 3, :] = value
+    y = permute_lanes(x[...], picks)
+    for q in range(4):
+        for i in range(19):
             for t in range(HELD):
-                row = 32 * part + 3 * (i // 2) + t
-                out[t, i : i + 1, 128 * q : 128 * q + 128] = y[row : row + 1, :]
+                r = 64 * q + 3 * i + t
+                out[t, i : i + 1, 128 * q : 128 * q + 128] = y[r : r + 1]
 
 
 def call(kernel, outs, scratch, *args, smem=0, limit=8 * 1024 * 1024):
@@ -417,10 +469,9 @@
         for step in range(STEPS - 1):
             zg = both_sides(zp, ("z", "core"), z_pairs)
             fc, zp = call(step_kernel, [state, sent], [state], fc, zg, nb3, wet)
-        zg = both_sides(zp, ("z", "core"), z_pairs)
-        back = call(last_kernel, (8, 32, 128), [state], fc, zg, nb3)
+        back = call(last_kernel, (chips, 48, 128), [], fc, nb3)
         home = lax.all_to_all(back, "z", 0, 0, tiled=True)
-        return call(unpack_kernel, (HELD, 19, 512), [(256, 128)], home)
+        return call(unpack_kernel, (HELD, 19, 512), [(256, 128)], home, neighbours)
 
     placed = (P(axes, None, None), P(axes), P(axes), P(axes), P(axes, None), P(axes, None))
     return jax.shard_map(

time: 90 us -> 85.2 us (0.947)
  blocking collectives: 77.6 us -> 72.1 us
    all_gather x5 -> x4, blocking collectives: 31 us -> 25.4 us  [both_sides(): y = lax.all_gather(x, names, axis_index_groups=groups)]
    all_to_all x1, blocking collectives: 11.1 us -> 13.4 us  [shards(): home = lax.all_to_all(back, 'z', 0, 0, tiled=True)]
    all_gather x5 -> x4, blocking collectives: 10.8 us -> 8.65 us  [both_sides(): return lax.all_gather(y, 'core')]
where the time goes in v2:
time: 85.2 us; the launch traced here: 84.8 us
  blocking collectives  72.1 us (85%)
  Pallas kernels  12.6 us (15%)
    all_gather x4, blocking collectives, both_sides(): y = lax.all_gather(x, names, axis_index_groups=groups)  25.4 us
    all_to_all x1, blocking collectives, shards(): planes = lax.all_to_all(packed, 'z', 0, 0, tiled=True)  20.7 us
    all_to_all x1, blocking collectives, shards(): home = lax.all_to_all(back, 'z', 0, 0, tiled=True)  13.4 us
    pallas_call x8, Pallas kernels, call(): pl.pallas_call(kernel, out_shape=shapes if many else shapes[0], in_specs=...  12.6 us
    all_gather x4, blocking collectives, both_sides(): return lax.all_gather(y, 'core')  8.65 us
    all_gather x1, blocking collectives, shards(): got = lax.all_gather(planes, 'core').reshape(16 * PACK, 128)  4.05 us

profile of v2, /device:TPU:1, one launch (start us, length us, event | category | flops | bytes accessed | tf_op | source)
XLA Modules:
  0.0 84.8 jit_solution(16114413413749931391)
XLA Ops:
  0.0 2.4 %shard_map.64 = f32[8,56,128]{2,1,0:T(8,128)} custom-call(s32[3]{0:T(128)} %keep.1, s32[2]{0:T(128)} %send.1, s32[2]{0:T(128)} %dest.1, s32[3,18]{1,0:T(4,128)} %nbr.3, f32[5,19,512]{2,1,0:T(8,128)} %pops.1, s32[3,512]{1,0:T(4,128)} %fluid.1), custom_call_target="tpu_custom_call" | custom-call | tf_op jit(solution)/shard_map/pallas_call | solution.py:422
  2.4 20.7 %all_to_all.10 = f32[8,56,128]{2,1,0:T(8,128)S(1)} all-to-all(f32[8,56,128]{2,1,0:T(8,128)} %shard_map.64), channel_id=1, replica_groups=mesh['wide'=32,'z'=8,'core'=2] {'z'}, dimensions={0} | all-to-all | bytes 458752 | tf_op jit(solution)/shard_map/all_to_all | solution.py:460
  23.1 4.1 %all-gather = f32[16,56,128]{2,1,0:T(8,128)S(1)} all-gather(f32[8,56,128]{2,1,0:T(8,128)S(1)} %all_to_all.10), channel_id=2, replica_groups=mesh['wide'=32,'z'=8,'core'=2] {'core'}, dimensions={0}, use_global_device_ids=true | all-gather | bytes 688128 | tf_op jit(solution)/shard_map/all_gather | solution.py:461
  27.1 1.4 %shard_map.65 = (f32[20,48,128]{2,1,0:T(8,128)S(1)}, f32[48,128]{1,0:T(8,128)S(1)}, f32[288,128]{1,0:T(8,128)S(1)}) custom-call(f32[896,128]{1,0:T(8,128)S(1)} %bitcast.13), custom_call_target="tpu_custom_call" | custom-call | tf_op jit(solution)/shard_map/pallas_call | solution.py:422
  28.5 8.6 %all-gather.1 = f32[576,128]{1,0:T(8,128)S(1)} all-gather(f32[288,128]{1,0:T(8,128)S(1)} %get-tuple-element.19), channel_id=3, replica_groups={{0,16},{2,18},{4,20},{6,22},{8,24},{10,26},{12,28},{14,30},{32,48},{34,..., dimensions={0}, use_global_device_ids=true | all-gather | bytes 442368 | tf_op jit(solution)/shard_map/all_gather | solution.py:451
  37.1 2.2 %all-gather.2 = f32[4,288,128]{2,1,0:T(8,128)S(1)} all-gather(f32[2,288,128]{2,1,0:T(8,128)S(1)} %bitcast.14), channel_id=4, replica_groups=mesh['wide'=32,'z'=8,'core'=2] {'core'}, dimensions={0}, use_global_device_ids=true | all-gather | bytes 884736 | tf_op jit(solution)/shard_map/all_gather | solution.py:452
  39.3 0.5 shard_map.66
  39.9 5.6 %all-gather.3 = f32[480,128]{1,0:T(8,128)S(1)} all-gather(f32[240,128]{1,0:T(8,128)S(1)} %get-tuple-element.21), channel_id=5, replica_groups={{0,2},{4,6},{8,10},{12,14},{3,5},{7,9},{11,13},{15,1},{16,18},{20,22},{..., dimensions={0}, use_global_device_ids=true | all-gather | bytes 368640 | tf_op jit(solution)/shard_map/all_gather | solution.py:451
  45.5 2.1 %all-gather.4 = f32[4,240,128]{2,1,0:T(8,128)S(1)} all-gather(f32[2,240,128]{2,1,0:T(8,128)S(1)} %bitcast.15), channel_id=6, replica_groups=mesh['wide'=32,'z'=8,'core'=2] {'core'}, dimensions={0}, use_global_device_ids=true | all-gather | bytes 737280 | tf_op jit(solution)/shard_map/all_gather | solution.py:452
  47.6 1.6 %shard_map.67 = (f32[19,48,128]{2,1,0:T(8,128)S(1)}, f32[240,128]{1,0:T(8,128)S(1)}) custom-call(f32[19,48,128]{2,1,0:T(8,128)S(1)} %get-tuple-element.20.fc, f32[2,2,240,128]{3,2,1,0:T(8,128)S(1)} %bitcast.11, f32[3,48,128]{2,1,0:T(8,128)S(1)} %get-tuple-element.22.nb3, f32[48,128]{1,0:T(8,128)S(1)} %get-tuple-element.23.fluid), custom_call_target="tpu_custom_call" | custom-call | tf_op jit(solution)/shard_map/pallas_call | solution.py:422
  49.2 5.6 %all-gather.5 = f32[480,128]{1,0:T(8,128)S(1)} all-gather(f32[240,128]{1,0:T(8,128)S(1)} %get-tuple-element.25), channel_id=7, replica_groups={{0,2},{4,6},{8,10},{12,14},{3,5},{7,9},{11,13},{15,1},{16,18},{20,22},{..., dimensions={0}, use_global_device_ids=true | all-gather | bytes 368640 | tf_op jit(solution)/shard_map/all_gather | solution.py:451
  54.8 2.1 %all-gather.6 = f32[4,240,128]{2,1,0:T(8,128)S(1)} all-gather(f32[2,240,128]{2,1,0:T(8,128)S(1)} %bitcast.16), channel_id=8, replica_groups=mesh['wide'=32,'z'=8,'core'=2] {'core'}, dimensions={0}, use_global_device_ids=true | all-gather | bytes 737280 | tf_op jit(solution)/shard_map/all_gather | solution.py:452
  57.0 1.7 %shard_map.68 = (f32[19,48,128]{2,1,0:T(8,128)S(1)}, f32[240,128]{1,0:T(8,128)S(1)}) custom-call(f32[19,48,128]{2,1,0:T(8,128)S(1)} %get-tuple-element.24.fc, f32[2,2,240,128]{3,2,1,0:T(8,128)S(1)} %bitcast.12, f32[3,48,128]{2,1,0:T(8,128)S(1)} %get-tuple-element.22.nb3, f32[48,128]{1,0:T(8,128)S(1)} %get-tuple-element.23.fluid), custom_call_target="tpu_custom_call" | custom-call | tf_op jit(solution)/shard_map/pallas_call | solution.py:422
  58.7 5.6 %all-gather.7 = f32[480,128]{1,0:T(8,128)S(1)} all-gather(f32[240,128]{1,0:T(8,128)S(1)} %get-tuple-element.27), channel_id=9, replica_groups={{0,2},{4,6},{8,10},{12,14},{3,5},{7,9},{11,13},{15,1},{16,18},{20,22},{..., dimensions={0}, use_global_device_ids=true | all-gather | bytes 368640 | tf_op jit(solution)/shard_map/all_gather | solution.py:451
  64.3 2.1 %all-gather.8 = f32[4,240,128]{2,1,0:T(8,128)S(1)} all-gather(f32[2,240,128]{2,1,0:T(8,128)S(1)} %bitcast.17), channel_id=10, replica_groups=mesh['wide'=32,'z'=8,'core'=2] {'core'}, dimensions={0}, use_global_device_ids=true | all-gather | bytes 737280 | tf_op jit(solution)/shard_map/all_gather | solution.py:452
  66.4 2.3 %shard_map.69 = (f32[19,48,128]{2,1,0:T(8,128)S(1)}, f32[240,128]{1,0:T(8,128)}) custom-call(f32[19,48,128]{2,1,0:T(8,128)S(1)} %get-tuple-element.26.fc, f32[2,2,240,128]{3,2,1,0:T(8,128)S(1)} %bitcast.10, f32[3,48,128]{2,1,0:T(8,128)S(1)} %get-tuple-element.22.nb3, f32[48,128]{1,0:T(8,128)S(1)} %get-tuple-element.23.fluid), custom_call_target="tpu_custom_call" | custom-call | tf_op jit(solution)/shard_map/pallas_call | solution.py:422
  68.7 1.3 %shard_map.70 = f32[8,48,128]{2,1,0:T(8,128)S(1)} custom-call(f32[19,48,128]{2,1,0:T(8,128)S(1)} %get-tuple-element.28.fc, f32[3,48,128]{2,1,0:T(8,128)S(1)} %get-tuple-element.22.nb3), custom_call_target="tpu_custom_call" | custom-call | tf_op jit(solution)/shard_map/pallas_call | solution.py:422
  70.0 0.0 copy-start
  70.0 13.4 %all_to_all.11.got = f32[8,48,128]{2,1,0:T(8,128)S(1)} all-to-all(f32[8,48,128]{2,1,0:T(8,128)S(1)} %shard_map.70), channel_id=1, replica_groups=mesh['wide'=32,'z'=8,'core'=2] {'z'}, dimensions={0} | all-to-all | bytes 393216 | tf_op jit(solution)/shard_map/all_to_all | solution.py:473
  83.4 0.0 copy-done
  83.4 1.4 %shard_map.71 = f32[3,19,512]{2,1,0:T(8,128)} custom-call(f32[8,48,128]{2,1,0:T(8,128)S(1)} %all_to_all.11.got, s32[3,18]{1,0:T(4,128)S(1)} %copy-done), custom_call_target="tpu_custom_call" | custom-call | tf_op jit(solution)/shard_map/pallas_call | solution.py:422
Async XLA Ops:
  70.0 13.4 %copy-start = (s32[3,18]{1,0:T(4,128)S(1)}, s32[3,18]{1,0:T(4,128)}, u32[]{:S(2)}) copy-start(s32[3,18]{1,0:T(4,128)} %nbr.3) | copy-start | bytes 652

commit v3 on v2

--- a/solution.py
+++ b/solution.py
@@ -7,7 +7,8 @@
 
 STEPS = 4
 HELD = 3
-ROWS = 48
+SLOTS = 48
+ROWS = 32
 PACK = 56
 PLANES = 8
 INTERPRET = False
@@ -178,43 +179,60 @@
 
 def place_kernel(got, st, nb, xp):
     tables = got[pl.ds(39, 16, stride=PACK), :]
-    row16 = iota((ROWS, 16), 0)
-    lane16 = iota((ROWS, 16), 1)
+    row16 = iota((SLOTS, 16), 0)
+    lane16 = iota((SLOTS, 16), 1)
     m16 = row16 // 3
     whose = (m16 % 2) * 8 + m16 // 2
     picks = (lane16 == whose).astype(F32).astype(BF16)
     mine = dot(picks, tables.astype(BF16))
-    lane, row = iota((ROWS, 128), 1), iota((ROWS, 128), 0)
+    lane, row = iota((SLOTS, 128), 1), iota((SLOTS, 128), 0)
     t = row % 3
     kept = jnp.sum(jnp.where(lane == 64 + t, mine, 0.0), axis=1, keepdims=True)
     eye = iota((16, 16), 0) == iota((16, 16), 1)
     lane_t = iota((16, 128), 1)
-    found = jnp.full((ROWS, 1), -4096, jnp.int32)
+    found = jnp.full((SLOTS, 1), -4096, jnp.int32)
     for j in range(2):
         column = jnp.sum(jnp.where(lane_t == 67 + j, tables, 0.0), axis=1, keepdims=True)
         diagonal = jnp.where(eye, column, 0.0).astype(BF16)
-        targets = dot(jnp.ones((ROWS, 16), BF16), diagonal)
+        targets = dot(jnp.ones((SLOTS, 16), BF16), diagonal)
         hit = targets == row16.astype(F32)
         where_from = jnp.where(hit, lane16 * PACK + 30 + 10 * j + 4096, 0)
         found = found + jnp.sum(where_from.astype(F32), axis=1, keepdims=True).astype(jnp.int32)
-    row1 = iota((ROWS, 1), 0)
+    row1 = iota((SLOTS, 1), 0)
     m1 = row1 // 3
     own = ((m1 % 2) * 8 + m1 // 2) * PACK + (row1 % 3) * 10
     source = jnp.where(kept >= 0.0, own, found)
+    occupied = (source >= 0).astype(F32)
+    ones = jnp.ones((ROWS, SLOTS), BF16)
+
+    def ranks(first, width):
+        r, slot = iota((SLOTS, width), 0), iota((SLOTS, width), 1) - first
+        earlier = dot(ones, jnp.where(r < slot, occupied, 0.0).astype(BF16))
+        full = dot(ones, jnp.where(r == slot, occupied, 0.0).astype(BF16))
+        return jnp.where(full > 0.5, earlier, -1.0)
+
+    rank = ranks(0, SLOTS)
+    picks = (rank == iota((ROWS, SLOTS), 0).astype(F32)).astype(F32).astype(BF16)
+    codes = jnp.zeros((SLOTS, 128), F32)
+    for k in range(3):
+        codes = jnp.where(t == k, pltpu.roll(mine, (128 - 74 - 18 * k) % 128, 1), codes)
+    codes = jnp.where(lane == 18, source.astype(F32), codes)
+    codes = jnp.where(lane == 19, own.astype(F32), codes)
+    codes = choose(picks, codes)
+    source = codes[:, 18:19].astype(jnp.int32)
+    own = codes[:, 19:20].astype(jnp.int32)
     wide_lane = iota((ROWS, 16 * PACK), 1)
     matrices = [(wide_lane == source + p).astype(F32) for p in range(10)]
     matrices.append((wide_lane == own + 9).astype(F32))
     full = choose(jnp.concatenate(matrices, axis=0).astype(BF16), got[...])
-    there = source >= 0
+    lane = iota((ROWS, 128), 1)
     middle = jnp.logical_and(lane >= 32, lane < 96)
     for i in range(19):
         value = full[ROWS * (i // 2) : ROWS * (i // 2) + ROWS]
         value = pltpu.roll(value, 32 if i % 2 == 0 else 96, 1)
-        st[i] = jnp.where(jnp.logical_and(there, middle), value, WEIGHTS[i])
+        st[i] = jnp.where(middle, value, WEIGHTS[i])
     st[19] = jnp.where(middle, pltpu.roll(full[10 * ROWS : 11 * ROWS], 96, 1), 0.0)
-    codes = jnp.zeros((ROWS, 128), F32)
-    for k in range(3):
-        codes = jnp.where(t == k, pltpu.roll(mine, (128 - 74 - 18 * k) % 128, 1), codes)
+    codes = jnp.where(lane < 18, codes, ranks(64, 128))
     nb[...] = codes
     to_right = ((lax.axis_index("wide") + lax.axis_index("core")) % 2) == 0
     for q in range(5):
@@ -245,9 +263,25 @@
             f[i] = value
         else:
             fluid[...] = value
-    nb3[0] = xg[left, 0, ROWS * 5 : ROWS * 6, :]
-    nb3[1] = nb[...]
-    nb3[2] = xg[right, 1, ROWS * 5 : ROWS * 6, :]
+    tables = [xg[left, 0, ROWS * 5 : ROWS * 6, :], nb[...], xg[right, 1, ROWS * 5 : ROWS * 6, :]]
+    back, ahead = lane < 0, lane < 0
+    for j in range(18):
+        if VELOCITY[j + 1][0] < 0:
+            back = jnp.logical_or(back, lane == j)
+        elif VELOCITY[j + 1][0] > 0:
+            ahead = jnp.logical_or(ahead, lane == j)
+    base = jnp.where(ahead, 2.0 * SLOTS, jnp.where(back, 0.0, 1.0 * SLOTS))
+    wanted = [jnp.where(table >= 0.0, table - base, -1.0) for table in tables]
+    done = [jnp.full((ROWS, 128), -1.0, F32) for _ in range(3)]
+    for slot in range(SLOTS):
+        rank = [table[:, 64 + slot : 65 + slot] for table in tables]
+        for g in range(3):
+            value = jnp.broadcast_to(rank[g], (ROWS, 128))
+            value = jnp.where(back, rank[g - 1] if g > 0 else -1.0, value)
+            value = jnp.where(ahead, rank[g + 1] if g < 2 else -1.0, value)
+            done[g] = jnp.where(wanted[g] == float(slot), value, done[g])
+    for g in range(3):
+        nb3[g] = jnp.where(lane < 18, done[g], tables[g])
     collide_all(f, fluid, fc)
     planes_to_send(fc, zp)
 
@@ -264,7 +298,7 @@
         if d == (0, 0, 0):
             return row1
         j = VELOCITY.index(d) - 1
-        return tables[g][:, j : j + 1] - (1 + d[0]) * ROWS
+        return tables[g][:, j : j + 1]
 
     def move(i, x, at_z):
         cx, cy, cz = VELOCITY[i]
@@ -334,7 +368,9 @@
     planes_to_send(fc_out, zp)
 
 
-def last_kernel(fc, nb3, out):
+def last_kernel(fc_in, zg, nb3, fluid, out, f, fc):
+    stream(fc_in, zg, nb3, f)
+    collide_all(f, fluid, fc)
     z = lax.axis_index("z")
     first = lax.axis_index("core") == 0
     lane = iota((ROWS, 128), 1)
@@ -343,11 +379,24 @@
     left += [move(i, fc[i], z == PLANES - 1) for i in UP] + [None]
     right = [move(i, fc[i], z == 0) for i in DOWN]
     right += [fc[OPPOSITE[i]] for i in UP + DOWN]
-    out[:, 40:48, :] = jnp.zeros((PLANES, 8, 128), F32)
+    left_rest = [WEIGHTS[i] for i in FLAT + UP] + [0.0]
+    right_rest = [WEIGHTS[i] for i in DOWN + UP + DOWN]
+    values = []
     for p in range(15):
         value = pltpu.roll(right[p], 32, 1)
         if left[p] is not None:
             value = jnp.where(lane < 64, pltpu.roll(left[p], 96, 1), value)
+        values.append(value)
+    lane, slot = iota((SLOTS, 128), 1), iota((SLOTS, 128), 0)
+    rank = jnp.broadcast_to(nb3[1, 0:1, :], (SLOTS, 128))
+    rank = jnp.sum(jnp.where(lane == 64 + slot, rank, 0.0), axis=1, keepdims=True)
+    picks = rank == iota((SLOTS, ROWS), 1).astype(F32)
+    spread = choose(picks.astype(F32).astype(BF16), jnp.concatenate(values, axis=1))
+    filled = rank >= 0.0
+    out[:, 40:48, :] = jnp.zeros((PLANES, 8, 128), F32)
+    for p in range(15):
+        rest = jnp.where(lane < 64, left_rest[p], right_rest[p])
+        value = jnp.where(filled, spread[:, 128 * p : 128 * p + 128], rest)
         for n in range(PLANES):
             a, b = value[6 * n : 6 * n + 3], value[6 * n + 3 : 6 * n + 6]
             out[n, 3 * p : 3 * p + 3, :] = jnp.where(first, a, b)
@@ -466,10 +515,11 @@
         fc, wet, nb3, zp = call(
             start_kernel, [state, (ROWS, 128), (3, ROWS, 128), sent], [state], st, nb, xg
         )
-        for step in range(STEPS - 1):
+        for step in range(STEPS - 2):
             zg = both_sides(zp, ("z", "core"), z_pairs)
             fc, zp = call(step_kernel, [state, sent], [state], fc, zg, nb3, wet)
-        back = call(last_kernel, (chips, 48, 128), [], fc, nb3)
+        zg = both_sides(zp, ("z", "core"), z_pairs)
+        back = call(last_kernel, (chips, 48, 128), [state, state], fc, zg, nb3, wet)
         home = lax.all_to_all(back, "z", 0, 0, tiled=True)
         return call(unpack_kernel, (HELD, 19, 512), [(256, 128)], home, neighbours)
 

time: 85.2 us -> 80.7 us (0.947)
  blocking collectives: 72.1 us -> 69.8 us
  Pallas kernels: 12.6 us -> 10.5 us
    pallas_call x8 -> x7, Pallas kernels: 12.6 us -> 10.5 us  [call(): pl.pallas_call(kernel, out_shape=shapes if many else shapes[0], in_specs=...]
    all_gather x4, blocking collectives: 25.4 us -> 23.5 us  [both_sides(): y = lax.all_gather(x, names, axis_index_groups=groups)]
where the time goes in v3:
time: 80.7 us; the launch traced here: 80.4 us
  blocking collectives  69.8 us (86%)
  Pallas kernels  10.5 us (13%)
    all_gather x4, blocking collectives, both_sides(): y = lax.all_gather(x, names, axis_index_groups=groups)  23.5 us
    all_to_all x1, blocking collectives, shards(): planes = lax.all_to_all(packed, 'z', 0, 0, tiled=True)  20.7 us
    all_to_all x1, blocking collectives, shards(): home = lax.all_to_all(back, 'z', 0, 0, tiled=True)  13.4 us
    pallas_call x7, Pallas kernels, call(): pl.pallas_call(kernel, out_shape=shapes if many else shapes[0], in_specs=...  10.5 us
    all_gather x4, blocking collectives, both_sides(): return lax.all_gather(y, 'core')  8.16 us
    all_gather x1, blocking collectives, shards(): got = lax.all_gather(planes, 'core').reshape(16 * PACK, 128)  4.05 us

profile of v3, /device:TPU:1, one launch (start us, length us, event | category | flops | bytes accessed | tf_op | source)
XLA Modules:
  0.0 80.4 jit_solution(16175262204103416937)
XLA Ops:
  0.0 2.4 %shard_map.64 = f32[8,56,128]{2,1,0:T(8,128)} custom-call(s32[3]{0:T(128)} %keep.1, s32[2]{0:T(128)} %send.1, s32[2]{0:T(128)} %dest.1, s32[3,18]{1,0:T(4,128)} %nbr.3, f32[5,19,512]{2,1,0:T(8,128)} %pops.1, s32[3,512]{1,0:T(4,128)} %fluid.1), custom_call_target="tpu_custom_call" | custom-call | tf_op jit(solution)/shard_map/pallas_call | solution.py:471
  2.4 20.7 %all_to_all.10 = f32[8,56,128]{2,1,0:T(8,128)S(1)} all-to-all(f32[8,56,128]{2,1,0:T(8,128)} %shard_map.64), channel_id=1, replica_groups=mesh['wide'=32,'z'=8,'core'=2] {'z'}, dimensions={0} | all-to-all | bytes 458752 | tf_op jit(solution)/shard_map/all_to_all | solution.py:509
  23.1 4.1 %all-gather = f32[16,56,128]{2,1,0:T(8,128)S(1)} all-gather(f32[8,56,128]{2,1,0:T(8,128)S(1)} %all_to_all.10), channel_id=2, replica_groups=mesh['wide'=32,'z'=8,'core'=2] {'core'}, dimensions={0}, use_global_device_ids=true | all-gather | bytes 688128 | tf_op jit(solution)/shard_map/all_gather | solution.py:510
  27.1 1.4 %shard_map.65 = (f32[20,32,128]{2,1,0:T(8,128)S(1)}, f32[32,128]{1,0:T(8,128)S(1)}, f32[192,128]{1,0:T(8,128)S(1)}) custom-call(f32[896,128]{1,0:T(8,128)S(1)} %bitcast.9), custom_call_target="tpu_custom_call" | custom-call | tf_op jit(solution)/shard_map/pallas_call | solution.py:471
  28.5 8.0 %all-gather.1 = f32[384,128]{1,0:T(8,128)S(1)} all-gather(f32[192,128]{1,0:T(8,128)S(1)} %get-tuple-element.18), channel_id=3, replica_groups={{0,16},{2,18},{4,20},{6,22},{8,24},{10,26},{12,28},{14,30},{32,48},{34,..., dimensions={0}, use_global_device_ids=true | all-gather | bytes 294912 | tf_op jit(solution)/shard_map/all_gather | solution.py:500
  36.6 2.1 %all-gather.2 = f32[4,192,128]{2,1,0:T(8,128)S(1)} all-gather(f32[2,192,128]{2,1,0:T(8,128)S(1)} %bitcast.14), channel_id=4, replica_groups=mesh['wide'=32,'z'=8,'core'=2] {'core'}, dimensions={0}, use_global_device_ids=true | all-gather | bytes 589824 | tf_op jit(solution)/shard_map/all_gather | solution.py:501
  38.7 1.1 %shard_map.66 = (f32[19,32,128]{2,1,0:T(8,128)S(1)}, f32[32,128]{1,0:T(8,128)S(1)}, f32[3,32,128]{2,1,0:T(8,128)S(1)}, f32[160,128]{1,0:T(8,128)S(1)}) custom-call(f32[20,32,128]{2,1,0:T(8,128)S(1)} %get-tuple-element.16.st, f32[32,128]{1,0:T(8,128)S(1)} %get-tuple-element.17.nb, f32[2,2,192,128]{3,2,1,0:T(8,128)S(1)} %bitcast.10), custom_call_target="tpu_custom_call" | custom-call | tf_op jit(solution)/shard_map/pallas_call | solution.py:471
  39.8 5.2 %all-gather.3 = f32[320,128]{1,0:T(8,128)S(1)} all-gather(f32[160,128]{1,0:T(8,128)S(1)} %get-tuple-element.20), channel_id=5, replica_groups={{0,2},{4,6},{8,10},{12,14},{3,5},{7,9},{11,13},{15,1},{16,18},{20,22},{..., dimensions={0}, use_global_device_ids=true | all-gather | bytes 245760 | tf_op jit(solution)/shard_map/all_gather | solution.py:500
  44.9 2.0 %all-gather.4 = f32[4,160,128]{2,1,0:T(8,128)S(1)} all-gather(f32[2,160,128]{2,1,0:T(8,128)S(1)} %bitcast.15), channel_id=6, replica_groups=mesh['wide'=32,'z'=8,'core'=2] {'core'}, dimensions={0}, use_global_device_ids=true | all-gather | bytes 491520 | tf_op jit(solution)/shard_map/all_gather | solution.py:501
  47.0 1.1 %shard_map.67 = (f32[19,32,128]{2,1,0:T(8,128)S(1)}, f32[160,128]{1,0:T(8,128)S(1)}) custom-call(f32[19,32,128]{2,1,0:T(8,128)S(1)} %get-tuple-element.19.fc, f32[2,2,160,128]{3,2,1,0:T(8,128)S(1)} %bitcast.11, f32[3,32,128]{2,1,0:T(8,128)S(1)} %get-tuple-element.21.nb3, f32[32,128]{1,0:T(8,128)S(1)} %get-tuple-element.22.fluid), custom_call_target="tpu_custom_call" | custom-call | tf_op jit(solution)/shard_map/pallas_call | solution.py:471
  48.1 5.2 %all-gather.5 = f32[320,128]{1,0:T(8,128)S(1)} all-gather(f32[160,128]{1,0:T(8,128)S(1)} %get-tuple-element.24), channel_id=7, replica_groups={{0,2},{4,6},{8,10},{12,14},{3,5},{7,9},{11,13},{15,1},{16,18},{20,22},{..., dimensions={0}, use_global_device_ids=true | all-gather | bytes 245760 | tf_op jit(solution)/shard_map/all_gather | solution.py:500
  53.3 2.0 %all-gather.6 = f32[4,160,128]{2,1,0:T(8,128)S(1)} all-gather(f32[2,160,128]{2,1,0:T(8,128)S(1)} %bitcast.16), channel_id=8, replica_groups=mesh['wide'=32,'z'=8,'core'=2] {'core'}, dimensions={0}, use_global_device_ids=true | all-gather | bytes 491520 | tf_op jit(solution)/shard_map/all_gather | solution.py:501
  55.3 1.1 %shard_map.68 = (f32[19,32,128]{2,1,0:T(8,128)S(1)}, f32[160,128]{1,0:T(8,128)S(1)}) custom-call(f32[19,32,128]{2,1,0:T(8,128)S(1)} %get-tuple-element.23.fc, f32[2,2,160,128]{3,2,1,0:T(8,128)S(1)} %bitcast.12, f32[3,32,128]{2,1,0:T(8,128)S(1)} %get-tuple-element.21.nb3, f32[32,128]{1,0:T(8,128)S(1)} %get-tuple-element.22.fluid), custom_call_target="tpu_custom_call" | custom-call | tf_op jit(solution)/shard_map/pallas_call | solution.py:471
  56.4 5.2 %all-gather.7 = f32[320,128]{1,0:T(8,128)S(1)} all-gather(f32[160,128]{1,0:T(8,128)S(1)} %get-tuple-element.26), channel_id=9, replica_groups={{0,2},{4,6},{8,10},{12,14},{3,5},{7,9},{11,13},{15,1},{16,18},{20,22},{..., dimensions={0}, use_global_device_ids=true | all-gather | bytes 245760 | tf_op jit(solution)/shard_map/all_gather | solution.py:500
  61.6 2.0 %all-gather.8 = f32[4,160,128]{2,1,0:T(8,128)S(1)} all-gather(f32[2,160,128]{2,1,0:T(8,128)S(1)} %bitcast.17), channel_id=10, replica_groups=mesh['wide'=32,'z'=8,'core'=2] {'core'}, dimensions={0}, use_global_device_ids=true | all-gather | bytes 491520 | tf_op jit(solution)/shard_map/all_gather | solution.py:501
  63.6 1.9 %shard_map.69 = f32[8,48,128]{2,1,0:T(8,128)S(1)} custom-call(f32[19,32,128]{2,1,0:T(8,128)S(1)} %get-tuple-element.25.fc_in, f32[2,2,160,128]{3,2,1,0:T(8,128)S(1)} %bitcast.13, f32[3,32,128]{2,1,0:T(8,128)S(1)} %get-tuple-element.21.nb3, f32[32,128]{1,0:T(8,128)S(1)} %get-tuple-element.22.fluid), custom_call_target="tpu_custom_call" | custom-call | tf_op jit(solution)/shard_map/pallas_call | solution.py:471
  65.6 0.0 copy-start
  65.6 13.4 %all_to_all.11.got = f32[8,48,128]{2,1,0:T(8,128)S(1)} all-to-all(f32[8,48,128]{2,1,0:T(8,128)S(1)} %shard_map.69), channel_id=1, replica_groups=mesh['wide'=32,'z'=8,'core'=2] {'z'}, dimensions={0} | all-to-all | bytes 393216 | tf_op jit(solution)/shard_map/all_to_all | solution.py:523
  78.9 0.0 copy-done
  78.9 1.4 %shard_map.70 = f32[3,19,512]{2,1,0:T(8,128)} custom-call(f32[8,48,128]{2,1,0:T(8,128)S(1)} %all_to_all.11.got, s32[3,18]{1,0:T(4,128)S(1)} %copy-done), custom_call_target="tpu_custom_call" | custom-call | tf_op jit(solution)/shard_map/pallas_call | solution.py:471
Async XLA Ops:
  65.6 13.4 %copy-start = (s32[3,18]{1,0:T(4,128)S(1)}, s32[3,18]{1,0:T(4,128)}, u32[]{:S(2)}) copy-start(s32[3,18]{1,0:T(4,128)} %nbr.3) | copy-start | bytes 652

commit v4 on v3

--- a/solution.py
+++ b/solution.py
@@ -9,7 +9,10 @@
 HELD = 3
 SLOTS = 48
 ROWS = 32
-PACK = 56
+PACK = 88
+KIND = 15
+TABLE_ROW = 59
+ARRAYS = 30
 PLANES = 8
 INTERPRET = False
 
@@ -139,21 +142,57 @@
             zp_ref[ROWS * k : ROWS * (k + 1), :] = fc_ref[DOWN[k]]
 
 
-def pack_kernel(keep, send, dest, nbr, pops, fluid, out, xa, xb):
+def pack_kernel(keep, send, dest, nbr, pops, fluid, out, xa, xb, raw):
     xa[...] = jnp.zeros_like(xa)
     xb[...] = jnp.zeros_like(xb)
+    raw[...] = jnp.ones_like(raw)
     for s in range(5):
         slot = jnp.maximum(keep[s] if s < HELD else send[s - HELD], 0)
+        xa[KIND * s : KIND * s + 15, :] = pops[slot, 0:15, :]
+        xb[KIND * s : KIND * s + 4, :] = pops[slot, 15:19, :]
         for i in range(19):
-            rows = slice(10 * s + i // 2, 10 * s + i // 2 + 1)
-            (xb if i % 2 else xa)[rows, :] = pops[slot, i : i + 1, :]
+            raw[i, s : s + 1, :] = pops[slot, i : i + 1, :]
+    walls = fluid[...].astype(F32)
     for t in range(HELD):
-        xb[10 * t + 9 : 10 * t + 10, :] = fluid[t : t + 1, :].astype(F32)
+        xb[KIND * t + 14 : KIND * t + 15, :] = walls[t : t + 1]
+    xa[85:88, :] = walls
+    xb[85:88, :] = walls
+    for j in range(2):
+        for k in range(5):
+            r = 75 + 5 * j + k
+            xa[r : r + 1, :] = raw[OPPOSITE[UP[k]], HELD + j : HELD + j + 1, :]
+            xb[r : r + 1, :] = raw[OPPOSITE[DOWN[k]], HELD + j : HELD + j + 1, :]
+    walls = jnp.concatenate([walls, jnp.ones((8 - HELD, 512), F32)], axis=0)
+    slots = jnp.full((8, 128), -1, jnp.int32)
+    for s in range(5):
+        slot = keep[s] if s < HELD else send[s - HELD]
+        slots = jnp.where(iota((8, 128), 0) == s, slot, slots)
+    for q in range(4):
+        cells = slice(128 * q, 128 * q + 128)
+        done = [jnp.where(slots >= 0, raw[i, :, cells], WEIGHTS[i]) for i in range(19)]
+        done = collide(done, walls[:, cells])
+        for k in range(5):
+            for s in range(5):
+                r = KIND * s + 4 + k
+                xb[r : r + 1, cells] = done[UP[k]][s : s + 1]
+                xb[r + 5 : r + 6, cells] = done[DOWN[k]][s : s + 1]
     k, n = iota((128, 128), 0), iota((128, 128), 1)
     picks = (n == (k % 8) * 16 + k // 8).astype(F32).astype(BF16)
     tiles = [x[:, 128 * q : 128 * q + 128] for x in (xa, xb) for q in range(4)]
     y = permute_lanes(jnp.concatenate(tiles, axis=0), picks)
     lane, row = iota((PACK, 128), 1), iota((PACK, 128), 0)
+    kind, late = row % KIND, row >= 75
+    rising = jnp.logical_and(jnp.logical_and(kind >= 4, kind < 9), jnp.logical_not(late))
+    falling = jnp.logical_or(jnp.logical_and(kind >= 9, kind < 14), late)
+    parts = []
+    for part in range(8):
+        piece = y[PACK * part : PACK * part + PACK]
+        if part < 4:
+            piece = jnp.where(late, pltpu.roll(piece, 16, 1), piece)
+        else:
+            moved = jnp.where(falling, pltpu.roll(piece, 112, 1), piece)
+            piece = jnp.where(rising, pltpu.roll(piece, 16, 1), moved)
+        parts.append(piece)
     values = [keep[t] for t in range(3)] + [dest[j] for j in range(2)]
     values = list(enumerate(values)) + [
         (10 + 18 * t + j, nbr[t, j]) for t in range(3) for j in range(18)
@@ -163,22 +202,21 @@
     for place, value in values:
         table = jnp.where(line == 64 + place, value, table)
     table = jnp.concatenate([table.astype(F32)] * (PACK // 8), axis=0)
-    marked = jnp.logical_and(row == 39, lane >= 64)
-    for z in range(8):
-        acc = table
+    marked = jnp.logical_and(row == TABLE_ROW, lane >= 64)
+    for z in range(PLANES):
+        acc = None
         for part in range(8):
-            piece = y[PACK * part : PACK * part + PACK]
             shift = (16 * part - 16 * z) % 128
-            piece = pltpu.roll(piece, shift, 1) if shift else piece
-            keep_mask = lane // 16 == part
-            if part >= 4:
-                keep_mask = jnp.logical_and(keep_mask, row != 39)
-            acc = jnp.where(keep_mask, piece, acc)
-        out[z] = jnp.where(jnp.logical_or(marked, lane < 128), acc, 0.0)
+            piece = pltpu.roll(parts[part], shift, 1) if shift else parts[part]
+            acc = piece if acc is None else jnp.where(lane // 16 == part, piece, acc)
+        out[z] = jnp.where(marked, table, acc)
 
 
 def place_kernel(got, st, nb, xp):
-    tables = got[pl.ds(39, 16, stride=PACK), :]
+    def of_all(row):
+        return got[pl.ds(row, 16, stride=PACK), :]
+
+    tables = of_all(TABLE_ROW)
     row16 = iota((SLOTS, 16), 0)
     lane16 = iota((SLOTS, 16), 1)
     m16 = row16 // 3
@@ -190,19 +228,19 @@
     kept = jnp.sum(jnp.where(lane == 64 + t, mine, 0.0), axis=1, keepdims=True)
     eye = iota((16, 16), 0) == iota((16, 16), 1)
     lane_t = iota((16, 128), 1)
-    found = jnp.full((SLOTS, 1), -4096, jnp.int32)
+    found = jnp.full((SLOTS, 1), -1.0, F32)
     for j in range(2):
         column = jnp.sum(jnp.where(lane_t == 67 + j, tables, 0.0), axis=1, keepdims=True)
         diagonal = jnp.where(eye, column, 0.0).astype(BF16)
         targets = dot(jnp.ones((SLOTS, 16), BF16), diagonal)
         hit = targets == row16.astype(F32)
-        where_from = jnp.where(hit, lane16 * PACK + 30 + 10 * j + 4096, 0)
-        found = found + jnp.sum(where_from.astype(F32), axis=1, keepdims=True).astype(jnp.int32)
+        where_from = jnp.where(hit, lane16 + 16 * (HELD + j) + 1, 0)
+        found = found + jnp.sum(where_from.astype(F32), axis=1, keepdims=True)
     row1 = iota((SLOTS, 1), 0)
     m1 = row1 // 3
-    own = ((m1 % 2) * 8 + m1 // 2) * PACK + (row1 % 3) * 10
+    own = ((m1 % 2) * 8 + m1 // 2 + (row1 % 3) * 16).astype(F32)
     source = jnp.where(kept >= 0.0, own, found)
-    occupied = (source >= 0).astype(F32)
+    occupied = (source >= 0.0).astype(F32)
     ones = jnp.ones((ROWS, SLOTS), BF16)
 
     def ranks(first, width):
@@ -216,41 +254,60 @@
     codes = jnp.zeros((SLOTS, 128), F32)
     for k in range(3):
         codes = jnp.where(t == k, pltpu.roll(mine, (128 - 74 - 18 * k) % 128, 1), codes)
-    codes = jnp.where(lane == 18, source.astype(F32), codes)
-    codes = jnp.where(lane == 19, own.astype(F32), codes)
+    codes = jnp.where(lane == 18, source, codes)
+    codes = jnp.where(lane == 19, own, codes)
     codes = choose(picks, codes)
-    source = codes[:, 18:19].astype(jnp.int32)
-    own = codes[:, 19:20].astype(jnp.int32)
-    wide_lane = iota((ROWS, 16 * PACK), 1)
-    matrices = [(wide_lane == source + p).astype(F32) for p in range(10)]
-    matrices.append((wide_lane == own + 9).astype(F32))
-    full = choose(jnp.concatenate(matrices, axis=0).astype(BF16), got[...])
+    source, own = codes[:, 18:19], codes[:, 19:20]
+
+    def one_hot(index, width):
+        return (iota((ROWS, width), 1).astype(F32) == index).astype(F32).astype(BF16)
+
+    def stacked(first, step, count):
+        return jnp.concatenate([of_all(first + step * s) for s in range(count)], axis=0)
+
+    lines = jnp.concatenate([stacked(p, KIND, 5) for p in range(KIND)], axis=1)
+    lines = choose(one_hot(source, 80), lines)
+    turned = jnp.concatenate([stacked(75 + k, 5, 2) for k in range(5)], axis=1)
+    turned = choose(one_hot(source - 48.0, 32), turned)
+    walls = jnp.concatenate([stacked(14, KIND, 3), stacked(85, 1, 3)], axis=1)
+    walls = choose(one_hot(own, SLOTS), walls)
+
+    def line(n):
+        value = lines[:, 128 * (n % KIND) : 128 * (n % KIND) + 128]
+        return pltpu.roll(value, 32 if n < KIND else 96, 1)
+
+    for i in range(19):
+        st[i] = line(i)
+    st[19] = pltpu.roll(walls[:, 0:128], 96, 1)
+    moved = source >= 48.0
+    for side in range(2):
+        wall = pltpu.roll(walls[:, 128:256], 96 if side else 32, 1) != 1.0
+        for k in range(5):
+            back = pltpu.roll(turned[:, 128 * k : 128 * k + 128], 96 if side else 32, 1)
+            arriving = line(19 + 5 * side + k)
+            st[20 + 5 * side + k] = jnp.where(jnp.logical_and(moved, wall), back, arriving)
     lane = iota((ROWS, 128), 1)
-    middle = jnp.logical_and(lane >= 32, lane < 96)
-    for i in range(19):
-        value = full[ROWS * (i // 2) : ROWS * (i // 2) + ROWS]
-        value = pltpu.roll(value, 32 if i % 2 == 0 else 96, 1)
-        st[i] = jnp.where(middle, value, WEIGHTS[i])
-    st[19] = jnp.where(middle, pltpu.roll(full[10 * ROWS : 11 * ROWS], 96, 1), 0.0)
     codes = jnp.where(lane < 18, codes, ranks(64, 128))
     nb[...] = codes
     to_right = ((lax.axis_index("wide") + lax.axis_index("core")) % 2) == 0
-    for q in range(5):
+    for q in range(8):
         acc = jnp.zeros((ROWS, 128), F32)
         for k in range(4):
+            if 4 * q + k >= ARRAYS:
+                continue
             value = st[4 * q + k]
             half = jnp.where(to_right, pltpu.roll(value, 64, 1), pltpu.roll(value, 96, 1))
             half = pltpu.roll(half, 32 * k, 1) if k else half
             acc = jnp.where(lane // 32 == k, half, acc)
         xp[ROWS * q : ROWS * q + ROWS, :] = acc
-    xp[ROWS * 5 : ROWS * 6, :] = codes
-
-
-def start_kernel(st, nb, xg, fc, fluid, nb3, zp, f):
+    xp[ROWS * 8 : ROWS * 9, :] = codes
+
+
+def start_kernel(st, nb, xg, fc_out, fluid, nb3, zp, f, fc, arriving):
     w = lax.axis_index("wide")
     lane = iota((ROWS, 128), 1)
     left, right = (w + 1) % 2, w % 2
-    for i in range(20):
+    for i in range(ARRAYS):
         rows = slice(ROWS * (i // 4), ROWS * (i // 4) + ROWS)
         from_left = xg[left, 0, rows, :]
         from_right = xg[right, 1, rows, :]
@@ -261,9 +318,12 @@
         value = jnp.where(lane < 32, from_left, jnp.where(lane < 96, st[i], from_right))
         if i < 19:
             f[i] = value
+        elif i == 19:
+            fluid[...] = value
         else:
-            fluid[...] = value
-    tables = [xg[left, 0, ROWS * 5 : ROWS * 6, :], nb[...], xg[right, 1, ROWS * 5 : ROWS * 6, :]]
+            arriving[i - 20] = value
+    last = slice(ROWS * 8, ROWS * 9)
+    tables = [xg[left, 0, last, :], nb[...], xg[right, 1, last, :]]
     back, ahead = lane < 0, lane < 0
     for j in range(18):
         if VELOCITY[j + 1][0] < 0:
@@ -283,7 +343,9 @@
     for g in range(3):
         nb3[g] = jnp.where(lane < 18, done[g], tables[g])
     collide_all(f, fluid, fc)
-    planes_to_send(fc, zp)
+    stream(fc, lambda k: arriving[k], lambda k: arriving[5 + k], nb3, f)
+    collide_all(f, fluid, fc_out)
+    planes_to_send(fc_out, zp)
 
 
 def passing(fc, nb3, segments):
@@ -347,29 +409,35 @@
     return move
 
 
-def stream(fc, zg, nb3, f):
+def stream(fc, from_below, from_above, nb3, f):
     z = lax.axis_index("z")
-    below, above = (z + 1) % 2, z % 2
     move = passing(fc, nb3, (0, 1, 2))
     for i in range(19):
         if i in UP:
-            k = UP.index(i)
-            f[i] = move(i, zg[below, 0, ROWS * k : ROWS * (k + 1), :], z == 0)
+            f[i] = move(i, from_below(UP.index(i)), z == 0)
         elif i in DOWN:
-            k = DOWN.index(i)
-            f[i] = move(i, zg[above, 1, ROWS * k : ROWS * (k + 1), :], z == PLANES - 1)
+            f[i] = move(i, from_above(DOWN.index(i)), z == PLANES - 1)
         else:
             f[i] = move(i, fc[i], None)
 
 
+def exchanged(zg):
+    z = lax.axis_index("z")
+    below, above = (z + 1) % 2, z % 2
+    return (
+        lambda k: zg[below, 0, ROWS * k : ROWS * (k + 1), :],
+        lambda k: zg[above, 1, ROWS * k : ROWS * (k + 1), :],
+    )
+
+
 def step_kernel(fc, zg, nb3, fluid, fc_out, zp, f):
-    stream(fc, zg, nb3, f)
+    stream(fc, *exchanged(zg), nb3, f)
     collide_all(f, fluid, fc_out)
     planes_to_send(fc_out, zp)
 
 
 def last_kernel(fc_in, zg, nb3, fluid, out, f, fc):
-    stream(fc_in, zg, nb3, f)
+    stream(fc_in, *exchanged(zg), nb3, f)
     collide_all(f, fluid, fc)
     z = lax.axis_index("z")
     first = lax.axis_index("core") == 0
@@ -502,20 +570,23 @@
 
     def shards(pops_in, keep_slot, send_slot, send_dest, neighbours, fluid):
         packed = call(
-            pack_kernel, (8, PACK, 128), [(PACK, 512), (PACK, 512)],
+            pack_kernel, (chips, PACK, 128), [(PACK, 512), (PACK, 512), (19, 8, 512)],
             keep_slot, send_slot, send_dest, neighbours, pops_in, fluid, smem=4,
             limit=None,
         )
         planes = lax.all_to_all(packed, "z", 0, 0, tiled=True)
-        got = lax.all_gather(planes, "core").reshape(16 * PACK, 128)
-        st, nb, xp = call(place_kernel, [(20, ROWS, 128), (ROWS, 128), (6 * ROWS, 128)], [], got)
+        got = lax.all_gather(planes, "core").reshape(group * PACK, 128)
+        st, nb, xp = call(
+            place_kernel, [(ARRAYS, ROWS, 128), (ROWS, 128), (9 * ROWS, 128)], [], got
+        )
         xg = both_sides(xp, axes, wide_pairs)
         state = (19, ROWS, 128)
         sent = (5 * ROWS, 128)
         fc, wet, nb3, zp = call(
-            start_kernel, [state, (ROWS, 128), (3, ROWS, 128), sent], [state], st, nb, xg
+            start_kernel, [state, (ROWS, 128), (3, ROWS, 128), sent],
+            [state, state, (10, ROWS, 128)], st, nb, xg,
         )
-        for step in range(STEPS - 2):
+        for step in range(STEPS - 3):
             zg = both_sides(zp, ("z", "core"), z_pairs)
             fc, zp = call(step_kernel, [state, sent], [state], fc, zg, nb3, wet)
         zg = both_sides(zp, ("z", "core"), z_pairs)

time: 80.7 us -> 77.9 us (0.965)
  blocking collectives: 69.8 us -> 66.3 us
    all_gather x4 -> x3, blocking collectives: 23.5 us -> 18.9 us  [both_sides(): y = lax.all_gather(x, names, axis_index_groups=groups)]
    all_to_all x1, blocking collectives: 20.7 us -> 23.9 us  [shards(): planes = lax.all_to_all(packed, 'z', 0, 0, tiled=True)]
    all_gather x4 -> x3, blocking collectives: 8.16 us -> 6.27 us  [both_sides(): return lax.all_gather(y, 'core')]
    pallas_call x7 -> x6, Pallas kernels: 10.5 us -> 11.2 us  [call(): pl.pallas_call(kernel, out_shape=shapes if many else shapes[0], in_specs=...]
where the time goes in v4:
time: 77.9 us; the launch traced here: 77.5 us
  blocking collectives  66.3 us (85%)
  Pallas kernels  11.2 us (14%)
    all_to_all x1, blocking collectives, shards(): planes = lax.all_to_all(packed, 'z', 0, 0, tiled=True)  23.9 us
    all_gather x3, blocking collectives, both_sides(): y = lax.all_gather(x, names, axis_index_groups=groups)  18.9 us
    all_to_all x1, blocking collectives, shards(): home = lax.all_to_all(back, 'z', 0, 0, tiled=True)  13.4 us
    pallas_call x6, Pallas kernels, call(): pl.pallas_call(kernel, out_shape=shapes if many else shapes[0], in_specs=...  11.2 us
    all_gather x3, blocking collectives, both_sides(): return lax.all_gather(y, 'core')  6.27 us
    all_gather x1, blocking collectives, shards(): got = lax.all_gather(planes, 'core').reshape(group * PACK, 128)  3.87 us

profile of v4, /device:TPU:1, one launch (start us, length us, event | category | flops | bytes accessed | tf_op | source)
XLA Modules:
  0.0 77.5 jit_solution(3350796182610630994)
XLA Ops:
  0.0 3.1 %shard_map.64 = f32[8,88,128]{2,1,0:T(8,128)} custom-call(s32[3]{0:T(128)} %keep.1, s32[2]{0:T(128)} %send.1, s32[2]{0:T(128)} %dest.1, s32[3,18]{1,0:T(4,128)} %nbr.3, f32[5,19,512]{2,1,0:T(8,128)} %pops.1, s32[3,512]{1,0:T(4,128)} %fluid.1), custom_call_target="tpu_custom_call" | custom-call | tf_op jit(solution)/shard_map/pallas_call | solution.py:539
  3.1 23.9 %all_to_all.10 = f32[8,88,128]{2,1,0:T(8,128)S(1)} all-to-all(f32[8,88,128]{2,1,0:T(8,128)} %shard_map.64), channel_id=1, replica_groups=mesh['wide'=32,'z'=8,'core'=2] {'z'}, dimensions={0} | all-to-all | bytes 720896 | tf_op jit(solution)/shard_map/all_to_all | solution.py:577
  26.9 3.9 %all-gather = f32[16,88,128]{2,1,0:T(8,128)S(1)} all-gather(f32[8,88,128]{2,1,0:T(8,128)S(1)} %all_to_all.10), channel_id=2, replica_groups=mesh['wide'=32,'z'=8,'core'=2] {'core'}, dimensions={0}, use_global_device_ids=true | all-gather | bytes 1081344 | tf_op jit(solution)/shard_map/all_gather | solution.py:578
  30.8 1.5 %shard_map.65 = (f32[30,32,128]{2,1,0:T(8,128)S(1)}, f32[32,128]{1,0:T(8,128)S(1)}, f32[288,128]{1,0:T(8,128)S(1)}) custom-call(f32[1408,128]{1,0:T(8,128)S(1)} %bitcast.7), custom_call_target="tpu_custom_call" | custom-call | tf_op jit(solution)/shard_map/pallas_call | solution.py:539
  32.3 8.6 %all-gather.1 = f32[576,128]{1,0:T(8,128)S(1)} all-gather(f32[288,128]{1,0:T(8,128)S(1)} %get-tuple-element.16), channel_id=3, replica_groups={{0,16},{2,18},{4,20},{6,22},{8,24},{10,26},{12,28},{14,30},{32,48},{34,..., dimensions={0}, use_global_device_ids=true | all-gather | bytes 442368 | tf_op jit(solution)/shard_map/all_gather | solution.py:568
  40.8 2.2 %all-gather.2 = f32[4,288,128]{2,1,0:T(8,128)S(1)} all-gather(f32[2,288,128]{2,1,0:T(8,128)S(1)} %bitcast.11), channel_id=4, replica_groups=mesh['wide'=32,'z'=8,'core'=2] {'core'}, dimensions={0}, use_global_device_ids=true | all-gather | bytes 884736 | tf_op jit(solution)/shard_map/all_gather | solution.py:569
  43.0 2.2 %shard_map.66 = (f32[19,32,128]{2,1,0:T(8,128)S(1)}, f32[32,128]{1,0:T(8,128)S(1)}, f32[3,32,128]{2,1,0:T(8,128)S(1)}, f32[160,128]{1,0:T(8,128)S(1)}) custom-call(f32[30,32,128]{2,1,0:T(8,128)S(1)} %get-tuple-element.14.st, f32[32,128]{1,0:T(8,128)S(1)} %get-tuple-element.15.nb, f32[2,2,288,128]{3,2,1,0:T(8,128)S(1)} %bitcast.8), custom_call_target="tpu_custom_call" | custom-call | tf_op jit(solution)/shard_map/pallas_call | solution.py:539
  45.3 5.2 %all-gather.3 = f32[320,128]{1,0:T(8,128)S(1)} all-gather(f32[160,128]{1,0:T(8,128)S(1)} %get-tuple-element.18), channel_id=5, replica_groups={{0,2},{4,6},{8,10},{12,14},{3,5},{7,9},{11,13},{15,1},{16,18},{20,22},{..., dimensions={0}, use_global_device_ids=true | all-gather | bytes 245760 | tf_op jit(solution)/shard_map/all_gather | solution.py:568
  50.4 2.0 %all-gather.4 = f32[4,160,128]{2,1,0:T(8,128)S(1)} all-gather(f32[2,160,128]{2,1,0:T(8,128)S(1)} %bitcast.12), channel_id=6, replica_groups=mesh['wide'=32,'z'=8,'core'=2] {'core'}, dimensions={0}, use_global_device_ids=true | all-gather | bytes 491520 | tf_op jit(solution)/shard_map/all_gather | solution.py:569
  52.5 1.1 %shard_map.67 = (f32[19,32,128]{2,1,0:T(8,128)S(1)}, f32[160,128]{1,0:T(8,128)S(1)}) custom-call(f32[19,32,128]{2,1,0:T(8,128)S(1)} %get-tuple-element.17.fc, f32[2,2,160,128]{3,2,1,0:T(8,128)S(1)} %bitcast.9, f32[3,32,128]{2,1,0:T(8,128)S(1)} %get-tuple-element.19.nb3, f32[32,128]{1,0:T(8,128)S(1)} %get-tuple-element.20.fluid), custom_call_target="tpu_custom_call" | custom-call | tf_op jit(solution)/shard_map/pallas_call | solution.py:539
  53.6 5.2 %all-gather.5 = f32[320,128]{1,0:T(8,128)S(1)} all-gather(f32[160,128]{1,0:T(8,128)S(1)} %get-tuple-element.22), channel_id=7, replica_groups={{0,2},{4,6},{8,10},{12,14},{3,5},{7,9},{11,13},{15,1},{16,18},{20,22},{..., dimensions={0}, use_global_device_ids=true | all-gather | bytes 245760 | tf_op jit(solution)/shard_map/all_gather | solution.py:568
  58.8 2.0 %all-gather.6 = f32[4,160,128]{2,1,0:T(8,128)S(1)} all-gather(f32[2,160,128]{2,1,0:T(8,128)S(1)} %bitcast.13), channel_id=8, replica_groups=mesh['wide'=32,'z'=8,'core'=2] {'core'}, dimensions={0}, use_global_device_ids=true | all-gather | bytes 491520 | tf_op jit(solution)/shard_map/all_gather | solution.py:569
  60.8 1.9 %shard_map.68 = f32[8,48,128]{2,1,0:T(8,128)S(1)} custom-call(f32[19,32,128]{2,1,0:T(8,128)S(1)} %get-tuple-element.21.fc_in, f32[2,2,160,128]{3,2,1,0:T(8,128)S(1)} %bitcast.10, f32[3,32,128]{2,1,0:T(8,128)S(1)} %get-tuple-element.19.nb3, f32[32,128]{1,0:T(8,128)S(1)} %get-tuple-element.20.fluid), custom_call_target="tpu_custom_call" | custom-call | tf_op jit(solution)/shard_map/pallas_call | solution.py:539
  62.7 0.0 copy-start
  62.8 13.4 %all_to_all.11.got = f32[8,48,128]{2,1,0:T(8,128)S(1)} all-to-all(f32[8,48,128]{2,1,0:T(8,128)S(1)} %shard_map.68), channel_id=1, replica_groups=mesh['wide'=32,'z'=8,'core'=2] {'z'}, dimensions={0} | all-to-all | bytes 393216 | tf_op jit(solution)/shard_map/all_to_all | solution.py:594
  76.1 0.0 copy-done
  76.1 1.4 %shard_map.69 = f32[3,19,512]{2,1,0:T(8,128)} custom-call(f32[8,48,128]{2,1,0:T(8,128)S(1)} %all_to_all.11.got, s32[3,18]{1,0:T(4,128)S(1)} %copy-done), custom_call_target="tpu_custom_call" | custom-call | tf_op jit(solution)/shard_map/pallas_call | solution.py:539
Async XLA Ops:
  62.7 13.4 %copy-start = (s32[3,18]{1,0:T(4,128)S(1)}, s32[3,18]{1,0:T(4,128)}, u32[]{:S(2)}) copy-start(s32[3,18]{1,0:T(4,128)} %nbr.3) | copy-start | bytes 652

commit v5 on v4

--- a/solution.py
+++ b/solution.py
@@ -303,7 +303,7 @@
     xp[ROWS * 8 : ROWS * 9, :] = codes
 
 
-def start_kernel(st, nb, xg, fc_out, fluid, nb3, zp, f, fc, arriving):
+def start_kernel(st, nb, xg, fc_out, fluid, nbt, zp, f, fc, arriving):
     w = lax.axis_index("wide")
     lane = iota((ROWS, 128), 1)
     left, right = (w + 1) % 2, w % 2
@@ -324,43 +324,42 @@
             arriving[i - 20] = value
     last = slice(ROWS * 8, ROWS * 9)
     tables = [xg[left, 0, last, :], nb[...], xg[right, 1, last, :]]
-    back, ahead = lane < 0, lane < 0
+    codes = jnp.where(lane < 36, pltpu.roll(tables[1], 18, 1), pltpu.roll(tables[2], 36, 1))
+    codes = jnp.where(lane < 18, tables[0], codes)
+    codes = jnp.where(lane < 54, codes, -1.0)
+    side = jnp.zeros((ROWS, 128), jnp.int32)
     for j in range(18):
-        if VELOCITY[j + 1][0] < 0:
-            back = jnp.logical_or(back, lane == j)
-        elif VELOCITY[j + 1][0] > 0:
-            ahead = jnp.logical_or(ahead, lane == j)
-    base = jnp.where(ahead, 2.0 * SLOTS, jnp.where(back, 0.0, 1.0 * SLOTS))
-    wanted = [jnp.where(table >= 0.0, table - base, -1.0) for table in tables]
-    done = [jnp.full((ROWS, 128), -1.0, F32) for _ in range(3)]
+        if VELOCITY[j + 1][0]:
+            side = jnp.where(lane % 18 == j, VELOCITY[j + 1][0], side)
+    wanted = jnp.where(codes >= 0.0, codes - ((1 + side) * SLOTS).astype(F32), -1.0)
+    slab = (lane // 18 + side)[0:8]
+    done = jnp.full((ROWS, 128), -1.0, F32)
     for slot in range(SLOTS):
-        rank = [table[:, 64 + slot : 65 + slot] for table in tables]
+        value = jnp.full((8, 128), -1.0, F32)
         for g in range(3):
-            value = jnp.broadcast_to(rank[g], (ROWS, 128))
-            value = jnp.where(back, rank[g - 1] if g > 0 else -1.0, value)
-            value = jnp.where(ahead, rank[g + 1] if g < 2 else -1.0, value)
-            done[g] = jnp.where(wanted[g] == float(slot), value, done[g])
-    for g in range(3):
-        nb3[g] = jnp.where(lane < 18, done[g], tables[g])
+            value = jnp.where(slab == g, tables[g][0:8, 64 + slot : 65 + slot], value)
+        value = jnp.concatenate([value] * (ROWS // 8), axis=0)
+        done = jnp.where(wanted == float(slot), value, done)
+    nbt[...] = jnp.where(lane < 54, done, tables[1])
     collide_all(f, fluid, fc)
-    stream(fc, lambda k: arriving[k], lambda k: arriving[5 + k], nb3, f)
+    stream(fc, lambda k: arriving[k], lambda k: arriving[5 + k], nbt, f)
     collide_all(f, fluid, fc_out)
     planes_to_send(fc_out, zp)
 
 
-def passing(fc, nb3, segments):
+def passing(fc, nbt, segments):
     lane = iota((ROWS, 128), 1)
     column, y = lane // 8, lane % 8
     segment = [column < 4, jnp.logical_and(column >= 4, column < 12), column >= 12]
     row1 = iota((ROWS, 1), 0)
     slots = iota((ROWS, ROWS), 1)
-    tables = {g: nb3[g].astype(jnp.int32) for g in segments}
+    table = nbt[...].astype(jnp.int32)
 
     def source_rows(g, d):
         if d == (0, 0, 0):
             return row1
         j = VELOCITY.index(d) - 1
-        return tables[g][:, j : j + 1]
+        return table[:, 18 * g + j : 18 * g + j + 1]
 
     def move(i, x, at_z):
         cx, cy, cz = VELOCITY[i]
@@ -409,9 +408,9 @@
     return move
 
 
-def stream(fc, from_below, from_above, nb3, f):
+def stream(fc, from_below, from_above, nbt, f):
     z = lax.axis_index("z")
-    move = passing(fc, nb3, (0, 1, 2))
+    move = passing(fc, nbt, (0, 1, 2))
     for i in range(19):
         if i in UP:
             f[i] = move(i, from_below(UP.index(i)), z == 0)
@@ -430,39 +429,45 @@
     )
 
 
-def step_kernel(fc, zg, nb3, fluid, fc_out, zp, f):
-    stream(fc, *exchanged(zg), nb3, f)
+def step_kernel(fc, zg, nbt, fluid, fc_out, zp, f):
+    stream(fc, *exchanged(zg), nbt, f)
     collide_all(f, fluid, fc_out)
     planes_to_send(fc_out, zp)
 
 
-def last_kernel(fc_in, zg, nb3, fluid, out, f, fc):
-    stream(fc_in, *exchanged(zg), nb3, f)
+def last_kernel(fc_in, zg, nbt, fluid, out, f, fc):
+    stream(fc_in, *exchanged(zg), nbt, f)
     collide_all(f, fluid, fc)
     z = lax.axis_index("z")
     first = lax.axis_index("core") == 0
     lane = iota((ROWS, 128), 1)
-    move = passing(fc, nb3, (1,))
-    left = [move(i, fc[i], None) for i in FLAT]
-    left += [move(i, fc[i], z == PLANES - 1) for i in UP] + [None]
-    right = [move(i, fc[i], z == 0) for i in DOWN]
-    right += [fc[OPPOSITE[i]] for i in UP + DOWN]
-    left_rest = [WEIGHTS[i] for i in FLAT + UP] + [0.0]
-    right_rest = [WEIGHTS[i] for i in DOWN + UP + DOWN]
+    move = passing(fc, nbt, (1,))
+    column, y = lane // 8, lane % 8
+    bare = [fc[OPPOSITE[i]] for i in range(19)]
+    up = [move(i, fc[i], z == PLANES - 1) for i in UP]
+    down = [move(i, fc[i], z == 0) for i in DOWN]
+    left = [move(i, fc[i], None) for i in FLAT] + up[:4]
+    right = up[4:] + down
+    right += [jnp.where(z == 0, bare[UP[k]], bare[DOWN[k]]) for k in range(5)]
+    edge = jnp.where(column == 5, pltpu.roll(bare[13], 8, 1), pltpu.roll(bare[12], 120, 1))
+    edge = jnp.where(column == 4, bare[11], jnp.where(column == 11, bare[14], edge))
+    right.append(edge)
+    edge = jnp.where(y == 1, pltpu.roll(bare[17], 1, 1), pltpu.roll(bare[16], 127, 1))
+    right.append(jnp.where(y == 0, bare[15], jnp.where(y == 7, bare[18], edge)))
+    left_rest = [WEIGHTS[i] for i in FLAT + UP[:4]]
+    right_rest = [WEIGHTS[i] for i in UP[4:] + DOWN + UP] + [WEIGHTS[18]] * 2
     values = []
-    for p in range(15):
+    for p in range(13):
         value = pltpu.roll(right[p], 32, 1)
-        if left[p] is not None:
-            value = jnp.where(lane < 64, pltpu.roll(left[p], 96, 1), value)
-        values.append(value)
+        values.append(jnp.where(lane < 64, pltpu.roll(left[p], 96, 1), value))
     lane, slot = iota((SLOTS, 128), 1), iota((SLOTS, 128), 0)
-    rank = jnp.broadcast_to(nb3[1, 0:1, :], (SLOTS, 128))
+    rank = jnp.broadcast_to(nbt[0:1, :], (SLOTS, 128))
     rank = jnp.sum(jnp.where(lane == 64 + slot, rank, 0.0), axis=1, keepdims=True)
     picks = rank == iota((SLOTS, ROWS), 1).astype(F32)
     spread = choose(picks.astype(F32).astype(BF16), jnp.concatenate(values, axis=1))
     filled = rank >= 0.0
-    out[:, 40:48, :] = jnp.zeros((PLANES, 8, 128), F32)
-    for p in range(15):
+    out[:, 32:40, :] = jnp.zeros((PLANES, 8, 128), F32)
+    for p in range(13):
         rest = jnp.where(lane < 64, left_rest[p], right_rest[p])
         value = jnp.where(filled, spread[:, 128 * p : 128 * p + 128], rest)
         for n in range(PLANES):
@@ -471,7 +476,7 @@
 
 
 def unpack_kernel(got, nbr, out, x):
-    lane, row = iota((48, 128), 1), iota((48, 128), 0)
+    lane, row = iota((40, 128), 1), iota((40, 128), 0)
     k, n = iota((128, 128), 0), iota((128, 128), 1)
     picks = (n == (k % 16) * 8 + k // 16).astype(F32).astype(BF16)
     place = iota((HELD, 128), 1)
@@ -490,7 +495,11 @@
     for q in range(4):
         a, b = gathered(q), gathered(4 + q)
         a = jnp.where(row >= 27, pltpu.roll(a, 16, 1), a)
-        b = jnp.where(row < 15, pltpu.roll(b, 112, 1), b)
+        falling = jnp.logical_and(row >= 3, row < 18)
+        b = jnp.where(falling, pltpu.roll(b, 112, 1), jnp.where(row < 3, pltpu.roll(b, 16, 1), b))
+        at_x, at_y = b[33:36], b[36:39]
+        edges = {11: at_x, 14: at_x, 13: pltpu.roll(at_x, 120, 1), 12: pltpu.roll(at_x, 8, 1)}
+        edges |= {15: at_y, 18: at_y, 17: pltpu.roll(at_y, 127, 1), 16: pltpu.roll(at_y, 1, 1)}
         here_x = 2 * q + (place % 16) // 8
 
         def missing(c):
@@ -511,14 +520,17 @@
             return found
 
         for i in range(19):
-            if i in UP:
-                j = 3 * UP.index(i)
-                bare = b[15 + j : 18 + j]
-                value = jnp.where(missing(VELOCITY[i]), bare, a[27 + j : 30 + j])
-            elif i in DOWN:
-                j = 3 * DOWN.index(i)
-                bare = b[30 + j : 33 + j]
-                value = jnp.where(missing(VELOCITY[i]), bare, b[j : j + 3])
+            if i in UP or i in DOWN:
+                k = (UP if i in UP else DOWN).index(i)
+                bare = b[18 + 3 * k : 21 + 3 * k]
+                if i in edges:
+                    bare = jnp.where(here_z == (0 if i in UP else 7), bare, edges[i])
+                j = 3 * k
+                if i in DOWN:
+                    value = b[3 + j : 6 + j]
+                else:
+                    value = a[27 + j : 30 + j] if k < 4 else b[0:3]
+                value = jnp.where(missing(VELOCITY[i]), bare, value)
             else:
                 j = 3 * FLAT.index(i)
                 value = a[j : j + 3]
@@ -569,10 +581,12 @@
         return lax.all_gather(y, "core")
 
     def shards(pops_in, keep_slot, send_slot, send_dest, neighbours, fluid):
+        held = (keep_slot, send_slot, send_dest, neighbours, pops_in, fluid)
+        if not INTERPRET:
+            held = [pltpu.with_memory_space_constraint(x, pltpu.HBM) for x in held]
         packed = call(
             pack_kernel, (chips, PACK, 128), [(PACK, 512), (PACK, 512), (19, 8, 512)],
-            keep_slot, send_slot, send_dest, neighbours, pops_in, fluid, smem=4,
-            limit=None,
+            *held, smem=4,
         )
         planes = lax.all_to_all(packed, "z", 0, 0, tiled=True)
         got = lax.all_gather(planes, "core").reshape(group * PACK, 128)
@@ -582,15 +596,15 @@
         xg = both_sides(xp, axes, wide_pairs)
         state = (19, ROWS, 128)
         sent = (5 * ROWS, 128)
-        fc, wet, nb3, zp = call(
-            start_kernel, [state, (ROWS, 128), (3, ROWS, 128), sent],
+        fc, wet, nbt, zp = call(
+            start_kernel, [state, (ROWS, 128), (ROWS, 128), sent],
             [state, state, (10, ROWS, 128)], st, nb, xg,
         )
         for step in range(STEPS - 3):
             zg = both_sides(zp, ("z", "core"), z_pairs)
-            fc, zp = call(step_kernel, [state, sent], [state], fc, zg, nb3, wet)
+            fc, zp = call(step_kernel, [state, sent], [state], fc, zg, nbt, wet)
         zg = both_sides(zp, ("z", "core"), z_pairs)
-        back = call(last_kernel, (chips, 48, 128), [state, state], fc, zg, nb3, wet)
+        back = call(last_kernel, (chips, 40, 128), [state, state], fc, zg, nbt, wet)
         home = lax.all_to_all(back, "z", 0, 0, tiled=True)
         return call(unpack_kernel, (HELD, 19, 512), [(256, 128)], home, neighbours)
 

time: 77.9 us -> 75.5 us (0.969)
  Pallas kernels: 11.2 us -> 9.97 us
  blocking collectives: 66.3 us -> 65.3 us
    pallas_call x6, Pallas kernels: 11.2 us -> 9.97 us  [call(): pl.pallas_call(kernel, out_shape=shapes if many else shapes[0], in_specs=...]
    all_to_all x1, blocking collectives: 13.4 us -> 12.6 us  [shards(): home = lax.all_to_all(back, 'z', 0, 0, tiled=True)]
where the time goes in v5:
time: 75.5 us; the launch traced here: 75.3 us
  blocking collectives  65.3 us (86%)
  Pallas kernels  9.97 us (13%)
    all_to_all x1, blocking collectives, shards(): planes = lax.all_to_all(packed, 'z', 0, 0, tiled=True)  23.7 us
    all_gather x3, blocking collectives, both_sides(): y = lax.all_gather(x, names, axis_index_groups=groups)  18.9 us
    all_to_all x1, blocking collectives, shards(): home = lax.all_to_all(back, 'z', 0, 0, tiled=True)  12.6 us
    pallas_call x6, Pallas kernels, call(): pl.pallas_call(kernel, out_shape=shapes if many else shapes[0], in_specs=...  9.97 us
    all_gather x3, blocking collectives, both_sides(): return lax.all_gather(y, 'core')  6.27 us
    all_gather x1, blocking collectives, shards(): got = lax.all_gather(planes, 'core').reshape(group * PACK, 128)  3.85 us

profile of v5, /device:TPU:1, one launch (start us, length us, event | category | flops | bytes accessed | tf_op | source)
XLA Modules:
  0.0 75.3 jit_solution(10543267502159328866)
XLA Ops:
  0.0 2.3 %shard_map.64 = f32[8,88,128]{2,1,0:T(8,128)S(1)} custom-call(s32[3]{0:T(128)} %keep.1, s32[2]{0:T(128)} %send.1, s32[2]{0:T(128)} %dest.1, s32[3,18]{1,0:T(4,128)} %nbr.3, f32[5,19,512]{2,1,0:T(8,128)} %pops.1, s32[3,512]{1,0:T(4,128)} %fluid.1), custom_call_target="tpu_custom_call" | custom-call | tf_op jit(solution)/shard_map/pallas_call | solution.py:551
  2.4 23.7 %all_to_all.10 = f32[8,88,128]{2,1,0:T(8,128)S(1)} all-to-all(f32[8,88,128]{2,1,0:T(8,128)S(1)} %shard_map.64), channel_id=1, replica_groups=mesh['wide'=32,'z'=8,'core'=2] {'z'}, dimensions={0} | all-to-all | bytes 720896 | tf_op jit(solution)/shard_map/all_to_all | solution.py:591
  26.0 3.9 %all-gather = f32[16,88,128]{2,1,0:T(8,128)S(1)} all-gather(f32[8,88,128]{2,1,0:T(8,128)S(1)} %all_to_all.10), channel_id=2, replica_groups=mesh['wide'=32,'z'=8,'core'=2] {'core'}, dimensions={0}, use_global_device_ids=true | all-gather | bytes 1081344 | tf_op jit(solution)/shard_map/all_gather | solution.py:592
  29.9 1.5 %shard_map.65 = (f32[30,32,128]{2,1,0:T(8,128)S(1)}, f32[32,128]{1,0:T(8,128)S(1)}, f32[288,128]{1,0:T(8,128)S(1)}) custom-call(f32[1408,128]{1,0:T(8,128)S(1)} %bitcast.7), custom_call_target="tpu_custom_call" | custom-call | tf_op jit(solution)/shard_map/pallas_call | solution.py:551
  31.3 8.6 %all-gather.1 = f32[576,128]{1,0:T(8,128)S(1)} all-gather(f32[288,128]{1,0:T(8,128)S(1)} %get-tuple-element.16), channel_id=3, replica_groups={{0,16},{2,18},{4,20},{6,22},{8,24},{10,26},{12,28},{14,30},{32,48},{34,..., dimensions={0}, use_global_device_ids=true | all-gather | bytes 442368 | tf_op jit(solution)/shard_map/all_gather | solution.py:580
  39.9 2.2 %all-gather.2 = f32[4,288,128]{2,1,0:T(8,128)S(1)} all-gather(f32[2,288,128]{2,1,0:T(8,128)S(1)} %bitcast.11), channel_id=4, replica_groups=mesh['wide'=32,'z'=8,'core'=2] {'core'}, dimensions={0}, use_global_device_ids=true | all-gather | bytes 884736 | tf_op jit(solution)/shard_map/all_gather | solution.py:581
  42.1 1.7 %shard_map.66 = (f32[19,32,128]{2,1,0:T(8,128)S(1)}, f32[32,128]{1,0:T(8,128)S(1)}, f32[32,128]{1,0:T(8,128)S(1)}, f32[160,128]{1,0:T(8,128)S(1)}) custom-call(f32[30,32,128]{2,1,0:T(8,128)S(1)} %get-tuple-element.14.st, f32[32,128]{1,0:T(8,128)S(1)} %get-tuple-element.15.nb, f32[2,2,288,128]{3,2,1,0:T(8,128)S(1)} %bitcast.8), custom_call_target="tpu_custom_call" | custom-call | tf_op jit(solution)/shard_map/pallas_call | solution.py:551
  43.8 5.2 %all-gather.3 = f32[320,128]{1,0:T(8,128)S(1)} all-gather(f32[160,128]{1,0:T(8,128)S(1)} %get-tuple-element.18), channel_id=5, replica_groups={{0,2},{4,6},{8,10},{12,14},{3,5},{7,9},{11,13},{15,1},{16,18},{20,22},{..., dimensions={0}, use_global_device_ids=true | all-gather | bytes 245760 | tf_op jit(solution)/shard_map/all_gather | solution.py:580
  49.0 2.0 %all-gather.4 = f32[4,160,128]{2,1,0:T(8,128)S(1)} all-gather(f32[2,160,128]{2,1,0:T(8,128)S(1)} %bitcast.12), channel_id=6, replica_groups=mesh['wide'=32,'z'=8,'core'=2] {'core'}, dimensions={0}, use_global_device_ids=true | all-gather | bytes 491520 | tf_op jit(solution)/shard_map/all_gather | solution.py:581
  51.0 1.1 %shard_map.67 = (f32[19,32,128]{2,1,0:T(8,128)S(1)}, f32[160,128]{1,0:T(8,128)S(1)}) custom-call(f32[19,32,128]{2,1,0:T(8,128)S(1)} %get-tuple-element.17.fc, f32[2,2,160,128]{3,2,1,0:T(8,128)S(1)} %bitcast.9, f32[32,128]{1,0:T(8,128)S(1)} %get-tuple-element.19.nbt, f32[32,128]{1,0:T(8,128)S(1)} %get-tuple-element.20.fluid), custom_call_target="tpu_custom_call" | custom-call | tf_op jit(solution)/shard_map/pallas_call | solution.py:551
  52.2 5.2 %all-gather.5 = f32[320,128]{1,0:T(8,128)S(1)} all-gather(f32[160,128]{1,0:T(8,128)S(1)} %get-tuple-element.22), channel_id=7, replica_groups={{0,2},{4,6},{8,10},{12,14},{3,5},{7,9},{11,13},{15,1},{16,18},{20,22},{..., dimensions={0}, use_global_device_ids=true | all-gather | bytes 245760 | tf_op jit(solution)/shard_map/all_gather | solution.py:580
  57.3 2.0 %all-gather.6 = f32[4,160,128]{2,1,0:T(8,128)S(1)} all-gather(f32[2,160,128]{2,1,0:T(8,128)S(1)} %bitcast.13), channel_id=8, replica_groups=mesh['wide'=32,'z'=8,'core'=2] {'core'}, dimensions={0}, use_global_device_ids=true | all-gather | bytes 491520 | tf_op jit(solution)/shard_map/all_gather | solution.py:581
  59.4 2.0 %shard_map.68 = f32[8,40,128]{2,1,0:T(8,128)S(1)} custom-call(f32[19,32,128]{2,1,0:T(8,128)S(1)} %get-tuple-element.21.fc_in, f32[2,2,160,128]{3,2,1,0:T(8,128)S(1)} %bitcast.10, f32[32,128]{1,0:T(8,128)S(1)} %get-tuple-element.19.nbt, f32[32,128]{1,0:T(8,128)S(1)} %get-tuple-element.20.fluid), custom_call_target="tpu_custom_call" | custom-call | tf_op jit(solution)/shard_map/pallas_call | solution.py:551
  61.3 0.0 copy-start
  61.3 12.6 %all_to_all.11.got = f32[8,40,128]{2,1,0:T(8,128)S(1)} all-to-all(f32[8,40,128]{2,1,0:T(8,128)S(1)} %shard_map.68), channel_id=1, replica_groups=mesh['wide'=32,'z'=8,'core'=2] {'z'}, dimensions={0} | all-to-all | bytes 327680 | tf_op jit(solution)/shard_map/all_to_all | solution.py:608
  73.9 0.0 copy-done
  73.9 1.4 %shard_map.69 = f32[3,19,512]{2,1,0:T(8,128)} custom-call(f32[8,40,128]{2,1,0:T(8,128)S(1)} %all_to_all.11.got, s32[3,18]{1,0:T(4,128)S(1)} %copy-done), custom_call_target="tpu_custom_call" | custom-call | tf_op jit(solution)/shard_map/pallas_call | solution.py:551
Async XLA Ops:
  61.3 12.6 %copy-start = (s32[3,18]{1,0:T(4,128)S(1)}, s32[3,18]{1,0:T(4,128)}, u32[]{:S(2)}) copy-start(s32[3,18]{1,0:T(4,128)} %nbr.3) | copy-start | bytes 652

commit v6 on v5

--- a/solution.py
+++ b/solution.py
@@ -65,6 +65,20 @@
     m = x.shape[0]
     y = dot(jnp.concatenate(split(x), axis=0), picks)
     return y[:m] + y[m : 2 * m] + y[2 * m :]
+
+
+def regroup(arrays):
+    arrays = list(arrays)
+    group = iota(arrays[0].shape, 1) // 16
+    for s in (1, 2, 4):
+        high = (group & s) != 0
+        for i in range(8):
+            if i & s:
+                continue
+            a, b = arrays[i], arrays[i | s]
+            arrays[i] = jnp.where(high, pltpu.roll(b, 16 * s, 1), a)
+            arrays[i | s] = jnp.where(high, b, pltpu.roll(a, 128 - 16 * s, 1))
+    return arrays
 
 
 def collide(f, fluid):
@@ -148,51 +162,43 @@
     raw[...] = jnp.ones_like(raw)
     for s in range(5):
         slot = jnp.maximum(keep[s] if s < HELD else send[s - HELD], 0)
-        xa[KIND * s : KIND * s + 15, :] = pops[slot, 0:15, :]
-        xb[KIND * s : KIND * s + 4, :] = pops[slot, 15:19, :]
-        for i in range(19):
-            raw[i, s : s + 1, :] = pops[slot, i : i + 1, :]
-    walls = fluid[...].astype(F32)
-    for t in range(HELD):
-        xb[KIND * t + 14 : KIND * t + 15, :] = walls[t : t + 1]
-    xa[85:88, :] = walls
-    xb[85:88, :] = walls
-    for j in range(2):
-        for k in range(5):
-            r = 75 + 5 * j + k
-            xa[r : r + 1, :] = raw[OPPOSITE[UP[k]], HELD + j : HELD + j + 1, :]
-            xb[r : r + 1, :] = raw[OPPOSITE[DOWN[k]], HELD + j : HELD + j + 1, :]
-    walls = jnp.concatenate([walls, jnp.ones((8 - HELD, 512), F32)], axis=0)
+        for q in range(4):
+            block = pops[slot, :, 128 * q : 128 * q + 128]
+            r = PACK * q + KIND * s
+            xa[r : r + 15, :] = block[0:15]
+            xb[r : r + 4, :] = block[15:19]
+            raw[pl.ds(152 * q + s, 19, stride=8), :] = block
+    walls = jnp.concatenate([fluid[...].astype(F32), jnp.ones((8 - HELD, 512), F32)], axis=0)
     slots = jnp.full((8, 128), -1, jnp.int32)
     for s in range(5):
         slot = keep[s] if s < HELD else send[s - HELD]
         slots = jnp.where(iota((8, 128), 0) == s, slot, slots)
     for q in range(4):
-        cells = slice(128 * q, 128 * q + 128)
-        done = [jnp.where(slots >= 0, raw[i, :, cells], WEIGHTS[i]) for i in range(19)]
-        done = collide(done, walls[:, cells])
+        wall = walls[:, 128 * q : 128 * q + 128]
+        r = PACK * q
+        xb[pl.ds(r + 14, HELD, stride=KIND), :] = wall[0:HELD]
+        xa[r + 85 : r + 88, :] = wall[0:HELD]
+        xb[r + 85 : r + 88, :] = wall[0:HELD]
+        own = [raw[152 * q + 8 * i : 152 * q + 8 * i + 8, :] for i in range(19)]
+        done = collide([jnp.where(slots >= 0, own[i], WEIGHTS[i]) for i in range(19)], wall)
         for k in range(5):
-            for s in range(5):
-                r = KIND * s + 4 + k
-                xb[r : r + 1, cells] = done[UP[k]][s : s + 1]
-                xb[r + 5 : r + 6, cells] = done[DOWN[k]][s : s + 1]
+            xa[pl.ds(r + 75 + k, 2, stride=5), :] = own[OPPOSITE[UP[k]]][HELD : HELD + 2]
+            xb[pl.ds(r + 75 + k, 2, stride=5), :] = own[OPPOSITE[DOWN[k]]][HELD : HELD + 2]
+            xb[pl.ds(r + 4 + k, 5, stride=KIND), :] = done[UP[k]][0:5]
+            xb[pl.ds(r + 9 + k, 5, stride=KIND), :] = done[DOWN[k]][0:5]
     k, n = iota((128, 128), 0), iota((128, 128), 1)
     picks = (n == (k % 8) * 16 + k // 8).astype(F32).astype(BF16)
-    tiles = [x[:, 128 * q : 128 * q + 128] for x in (xa, xb) for q in range(4)]
-    y = permute_lanes(jnp.concatenate(tiles, axis=0), picks)
+    y = permute_lanes(jnp.concatenate([xa[...], xb[...]], axis=0), picks)
     lane, row = iota((PACK, 128), 1), iota((PACK, 128), 0)
     kind, late = row % KIND, row >= 75
     rising = jnp.logical_and(jnp.logical_and(kind >= 4, kind < 9), jnp.logical_not(late))
     falling = jnp.logical_or(jnp.logical_and(kind >= 9, kind < 14), late)
-    parts = []
-    for part in range(8):
-        piece = y[PACK * part : PACK * part + PACK]
-        if part < 4:
-            piece = jnp.where(late, pltpu.roll(piece, 16, 1), piece)
-        else:
-            moved = jnp.where(falling, pltpu.roll(piece, 112, 1), piece)
-            piece = jnp.where(rising, pltpu.roll(piece, 16, 1), moved)
-        parts.append(piece)
+    second = lane >= 64
+    rising = jnp.logical_or(
+        jnp.logical_and(second, rising), jnp.logical_and(late, jnp.logical_not(second))
+    )
+    falling = jnp.logical_and(second, falling)
+    parts = regroup([y[PACK * part : PACK * part + PACK] for part in range(8)])
     values = [keep[t] for t in range(3)] + [dest[j] for j in range(2)]
     values = list(enumerate(values)) + [
         (10 + 18 * t + j, nbr[t, j]) for t in range(3) for j in range(18)
@@ -204,12 +210,9 @@
     table = jnp.concatenate([table.astype(F32)] * (PACK // 8), axis=0)
     marked = jnp.logical_and(row == TABLE_ROW, lane >= 64)
     for z in range(PLANES):
-        acc = None
-        for part in range(8):
-            shift = (16 * part - 16 * z) % 128
-            piece = pltpu.roll(parts[part], shift, 1) if shift else parts[part]
-            acc = piece if acc is None else jnp.where(lane // 16 == part, piece, acc)
-        out[z] = jnp.where(marked, table, acc)
+        value = jnp.where(falling, parts[(z + 1) % PLANES], parts[z])
+        value = jnp.where(rising, parts[(z - 1) % PLANES], value)
+        out[z] = jnp.where(marked, table, value)
 
 
 def place_kernel(got, st, nb, xp):
@@ -351,15 +354,17 @@
     lane = iota((ROWS, 128), 1)
     column, y = lane // 8, lane % 8
     segment = [column < 4, jnp.logical_and(column >= 4, column < 12), column >= 12]
-    row1 = iota((ROWS, 1), 0)
     slots = iota((ROWS, ROWS), 1)
     table = nbt[...].astype(jnp.int32)
+    known = {}
 
     def source_rows(g, d):
         if d == (0, 0, 0):
-            return row1
-        j = VELOCITY.index(d) - 1
-        return table[:, 18 * g + j : 18 * g + j + 1]
+            return iota((ROWS, 128), 0)
+        j = 18 * g + VELOCITY.index(d) - 1
+        if j not in known:
+            known[j] = jnp.broadcast_to(table[:, j : j + 1], (ROWS, 128))
+        return known[j]
 
     def move(i, x, at_z):
         cx, cy, cz = VELOCITY[i]
@@ -394,7 +399,7 @@
                     parts.append((mask, rows))
         if not parts:
             return moved
-        picks = [(rows == slots).astype(F32) for _, rows in parts]
+        picks = [(rows[:, :ROWS] == slots).astype(F32) for _, rows in parts]
         taken = choose(jnp.concatenate(picks, axis=0).astype(BF16), moved)
         bounced = fc[OPPOSITE[i]]
         out = moved
@@ -475,7 +480,7 @@
             out[n, 3 * p : 3 * p + 3, :] = jnp.where(first, a, b)
 
 
-def unpack_kernel(got, nbr, out, x):
+def unpack_kernel(got, nbr, out, x, y):
     lane, row = iota((40, 128), 1), iota((40, 128), 0)
     k, n = iota((128, 128), 0), iota((128, 128), 1)
     picks = (n == (k % 16) * 8 + k // 16).astype(F32).astype(BF16)
@@ -484,16 +489,9 @@
     absent = [nbr[:, j : j + 1] < 0 for j in range(18)]
     x[...] = jnp.zeros_like(x)
 
-    def gathered(part):
-        acc = None
-        for z in range(PLANES):
-            shift = (16 * z - 16 * part) % 128
-            piece = pltpu.roll(got[z], shift, 1) if shift else got[z]
-            acc = piece if acc is None else jnp.where(lane // 16 == z, piece, acc)
-        return acc
-
+    tiles = regroup([got[z] for z in range(PLANES)])
     for q in range(4):
-        a, b = gathered(q), gathered(4 + q)
+        a, b = tiles[q], tiles[4 + q]
         a = jnp.where(row >= 27, pltpu.roll(a, 16, 1), a)
         falling = jnp.logical_and(row >= 3, row < 18)
         b = jnp.where(falling, pltpu.roll(b, 112, 1), jnp.where(row < 3, pltpu.roll(b, 16, 1), b))
@@ -535,12 +533,10 @@
                 j = 3 * FLAT.index(i)
                 value = a[j : j + 3]
             x[64 * q + 3 * i : 64 * q + 3 * i + 3, :] = value
-    y = permute_lanes(x[...], picks)
+    y[...] = permute_lanes(x[...], picks)
     for q in range(4):
-        for i in range(19):
-            for t in range(HELD):
-                r = 64 * q + 3 * i + t
-                out[t, i : i + 1, 128 * q : 128 * q + 128] = y[r : r + 1]
+        for t in range(HELD):
+            out[t, :, 128 * q : 128 * q + 128] = y[pl.ds(64 * q + t, 19, stride=3), :]
 
 
 def call(kernel, outs, scratch, *args, smem=0, limit=8 * 1024 * 1024):
@@ -585,7 +581,7 @@
         if not INTERPRET:
             held = [pltpu.with_memory_space_constraint(x, pltpu.HBM) for x in held]
         packed = call(
-            pack_kernel, (chips, PACK, 128), [(PACK, 512), (PACK, 512), (19, 8, 512)],
+            pack_kernel, (chips, PACK, 128), [(4 * PACK, 128), (4 * PACK, 128), (4 * 152, 128)],
             *held, smem=4,
         )
         planes = lax.all_to_all(packed, "z", 0, 0, tiled=True)
@@ -606,7 +602,7 @@
         zg = both_sides(zp, ("z", "core"), z_pairs)
         back = call(last_kernel, (chips, 40, 128), [state, state], fc, zg, nbt, wet)
         home = lax.all_to_all(back, "z", 0, 0, tiled=True)
-        return call(unpack_kernel, (HELD, 19, 512), [(256, 128)], home, neighbours)
+        return call(unpack_kernel, (HELD, 19, 512), [(256, 128)] * 2, home, neighbours)
 
     placed = (P(axes, None, None), P(axes), P(axes), P(axes), P(axes, None), P(axes, None))
     return jax.shard_map(

time: 75.5 us -> 74.4 us (0.985)
  Pallas kernels: 9.97 us -> 8.89 us
    pallas_call x6, Pallas kernels: 9.97 us -> 8.89 us  [call(): pl.pallas_call(kernel, out_shape=shapes if many else shapes[0], in_specs=...]
where the time goes in v6:
time: 74.4 us; the launch traced here: 74.2 us
  blocking collectives  65.2 us (88%)
  Pallas kernels  8.89 us (12%)
    all_to_all x1, blocking collectives, shards(): planes = lax.all_to_all(packed, 'z', 0, 0, tiled=True)  23.7 us
    all_gather x3, blocking collectives, both_sides(): y = lax.all_gather(x, names, axis_index_groups=groups)  18.9 us
    all_to_all x1, blocking collectives, shards(): home = lax.all_to_all(back, 'z', 0, 0, tiled=True)  12.5 us
    pallas_call x6, Pallas kernels, call(): pl.pallas_call(kernel, out_shape=shapes if many else shapes[0], in_specs=...  8.89 us
    all_gather x3, blocking collectives, both_sides(): return lax.all_gather(y, 'core')  6.27 us
    all_gather x1, blocking collectives, shards(): got = lax.all_gather(planes, 'core').reshape(group * PACK, 128)  3.85 us

profile of v6, /device:TPU:1, one launch (start us, length us, event | category | flops | bytes accessed | tf_op | source)
XLA Modules:
  0.0 74.2 jit_solution(7846597487513255521)
XLA Ops:
  0.0 1.8 %shard_map.64 = f32[8,88,128]{2,1,0:T(8,128)S(1)} custom-call(s32[3]{0:T(128)} %keep.1, s32[2]{0:T(128)} %send.1, s32[2]{0:T(128)} %dest.1, s32[3,18]{1,0:T(4,128)} %nbr.3, f32[5,19,512]{2,1,0:T(8,128)} %pops.1, s32[3,512]{1,0:T(4,128)} %fluid.1), custom_call_target="tpu_custom_call" | custom-call | tf_op jit(solution)/shard_map/pallas_call | solution.py:547
  1.8 23.7 %all_to_all.10 = f32[8,88,128]{2,1,0:T(8,128)S(1)} all-to-all(f32[8,88,128]{2,1,0:T(8,128)S(1)} %shard_map.64), channel_id=1, replica_groups=mesh['wide'=32,'z'=8,'core'=2] {'z'}, dimensions={0} | all-to-all | bytes 720896 | tf_op jit(solution)/shard_map/all_to_all | solution.py:587
  25.5 3.9 %all-gather = f32[16,88,128]{2,1,0:T(8,128)S(1)} all-gather(f32[8,88,128]{2,1,0:T(8,128)S(1)} %all_to_all.10), channel_id=2, replica_groups=mesh['wide'=32,'z'=8,'core'=2] {'core'}, dimensions={0}, use_global_device_ids=true | all-gather | bytes 1081344 | tf_op jit(solution)/shard_map/all_gather | solution.py:588
  29.3 1.5 %shard_map.65 = (f32[30,32,128]{2,1,0:T(8,128)S(1)}, f32[32,128]{1,0:T(8,128)S(1)}, f32[288,128]{1,0:T(8,128)S(1)}) custom-call(f32[1408,128]{1,0:T(8,128)S(1)} %bitcast.7), custom_call_target="tpu_custom_call" | custom-call | tf_op jit(solution)/shard_map/pallas_call | solution.py:547
  30.8 8.6 %all-gather.1 = f32[576,128]{1,0:T(8,128)S(1)} all-gather(f32[288,128]{1,0:T(8,128)S(1)} %get-tuple-element.16), channel_id=3, replica_groups={{0,16},{2,18},{4,20},{6,22},{8,24},{10,26},{12,28},{14,30},{32,48},{34,..., dimensions={0}, use_global_device_ids=true | all-gather | bytes 442368 | tf_op jit(solution)/shard_map/all_gather | solution.py:576
  39.3 2.2 %all-gather.2 = f32[4,288,128]{2,1,0:T(8,128)S(1)} all-gather(f32[2,288,128]{2,1,0:T(8,128)S(1)} %bitcast.11), channel_id=4, replica_groups=mesh['wide'=32,'z'=8,'core'=2] {'core'}, dimensions={0}, use_global_device_ids=true | all-gather | bytes 884736 | tf_op jit(solution)/shard_map/all_gather | solution.py:577
  41.6 1.7 %shard_map.66 = (f32[19,32,128]{2,1,0:T(8,128)S(1)}, f32[32,128]{1,0:T(8,128)S(1)}, f32[32,128]{1,0:T(8,128)S(1)}, f32[160,128]{1,0:T(8,128)S(1)}) custom-call(f32[30,32,128]{2,1,0:T(8,128)S(1)} %get-tuple-element.14.st, f32[32,128]{1,0:T(8,128)S(1)} %get-tuple-element.15.nb, f32[2,2,288,128]{3,2,1,0:T(8,128)S(1)} %bitcast.8), custom_call_target="tpu_custom_call" | custom-call | tf_op jit(solution)/shard_map/pallas_call | solution.py:547
  43.2 5.2 %all-gather.3 = f32[320,128]{1,0:T(8,128)S(1)} all-gather(f32[160,128]{1,0:T(8,128)S(1)} %get-tuple-element.18), channel_id=5, replica_groups={{0,2},{4,6},{8,10},{12,14},{3,5},{7,9},{11,13},{15,1},{16,18},{20,22},{..., dimensions={0}, use_global_device_ids=true | all-gather | bytes 245760 | tf_op jit(solution)/shard_map/all_gather | solution.py:576
  48.4 2.0 %all-gather.4 = f32[4,160,128]{2,1,0:T(8,128)S(1)} all-gather(f32[2,160,128]{2,1,0:T(8,128)S(1)} %bitcast.12), channel_id=6, replica_groups=mesh['wide'=32,'z'=8,'core'=2] {'core'}, dimensions={0}, use_global_device_ids=true | all-gather | bytes 491520 | tf_op jit(solution)/shard_map/all_gather | solution.py:577
  50.4 1.0 %shard_map.67 = (f32[19,32,128]{2,1,0:T(8,128)S(1)}, f32[160,128]{1,0:T(8,128)S(1)}) custom-call(f32[19,32,128]{2,1,0:T(8,128)S(1)} %get-tuple-element.17.fc, f32[2,2,160,128]{3,2,1,0:T(8,128)S(1)} %bitcast.9, f32[32,128]{1,0:T(8,128)S(1)} %get-tuple-element.19.nbt, f32[32,128]{1,0:T(8,128)S(1)} %get-tuple-element.20.fluid), custom_call_target="tpu_custom_call" | custom-call | tf_op jit(solution)/shard_map/pallas_call | solution.py:547
  51.5 5.2 %all-gather.5 = f32[320,128]{1,0:T(8,128)S(1)} all-gather(f32[160,128]{1,0:T(8,128)S(1)} %get-tuple-element.22), channel_id=7, replica_groups={{0,2},{4,6},{8,10},{12,14},{3,5},{7,9},{11,13},{15,1},{16,18},{20,22},{..., dimensions={0}, use_global_device_ids=true | all-gather | bytes 245760 | tf_op jit(solution)/shard_map/all_gather | solution.py:576
  56.6 2.0 %all-gather.6 = f32[4,160,128]{2,1,0:T(8,128)S(1)} all-gather(f32[2,160,128]{2,1,0:T(8,128)S(1)} %bitcast.13), channel_id=8, replica_groups=mesh['wide'=32,'z'=8,'core'=2] {'core'}, dimensions={0}, use_global_device_ids=true | all-gather | bytes 491520 | tf_op jit(solution)/shard_map/all_gather | solution.py:577
  58.7 1.8 %shard_map.68 = f32[8,40,128]{2,1,0:T(8,128)S(1)} custom-call(f32[19,32,128]{2,1,0:T(8,128)S(1)} %get-tuple-element.21.fc_in, f32[2,2,160,128]{3,2,1,0:T(8,128)S(1)} %bitcast.10, f32[32,128]{1,0:T(8,128)S(1)} %get-tuple-element.19.nbt, f32[32,128]{1,0:T(8,128)S(1)} %get-tuple-element.20.fluid), custom_call_target="tpu_custom_call" | custom-call | tf_op jit(solution)/shard_map/pallas_call | solution.py:547
  60.4 0.0 copy-start
  60.4 12.5 %all_to_all.11.got = f32[8,40,128]{2,1,0:T(8,128)S(1)} all-to-all(f32[8,40,128]{2,1,0:T(8,128)S(1)} %shard_map.68), channel_id=1, replica_groups=mesh['wide'=32,'z'=8,'core'=2] {'z'}, dimensions={0} | all-to-all | bytes 327680 | tf_op jit(solution)/shard_map/all_to_all | solution.py:604
  73.0 0.0 copy-done
  73.0 1.2 %shard_map.69 = f32[3,19,512]{2,1,0:T(8,128)} custom-call(f32[8,40,128]{2,1,0:T(8,128)S(1)} %all_to_all.11.got, s32[3,18]{1,0:T(4,128)S(1)} %copy-done), custom_call_target="tpu_custom_call" | custom-call | tf_op jit(solution)/shard_map/pallas_call | solution.py:547
Async XLA Ops:
  60.4 12.6 %copy-start = (s32[3,18]{1,0:T(4,128)S(1)}, s32[3,18]{1,0:T(4,128)}, u32[]{:S(2)}) copy-start(s32[3,18]{1,0:T(4,128)} %nbr.3) | copy-start | bytes 652

commit v7 on v6

--- a/solution.py
+++ b/solution.py
@@ -188,7 +188,7 @@
             xb[pl.ds(r + 9 + k, 5, stride=KIND), :] = done[DOWN[k]][0:5]
     k, n = iota((128, 128), 0), iota((128, 128), 1)
     picks = (n == (k % 8) * 16 + k // 8).astype(F32).astype(BF16)
-    y = permute_lanes(jnp.concatenate([xa[...], xb[...]], axis=0), picks)
+    y = permute_lanes(jnp.concatenate([xa[0 : 4 * PACK, :], xb[0 : 4 * PACK, :]], axis=0), picks)
     lane, row = iota((PACK, 128), 1), iota((PACK, 128), 0)
     kind, late = row % KIND, row >= 75
     rising = jnp.logical_and(jnp.logical_and(kind >= 4, kind < 9), jnp.logical_not(late))
@@ -533,7 +533,8 @@
                 j = 3 * FLAT.index(i)
                 value = a[j : j + 3]
             x[64 * q + 3 * i : 64 * q + 3 * i + 3, :] = value
-    y[...] = permute_lanes(x[...], picks)
+    y[0:256, :] = permute_lanes(x[...], picks)
+    y[256:272, :] = jnp.zeros((16, 128), F32)
     for q in range(4):
         for t in range(HELD):
             out[t, :, 128 * q : 128 * q + 128] = y[pl.ds(64 * q + t, 19, stride=3), :]
@@ -581,7 +582,7 @@
         if not INTERPRET:
             held = [pltpu.with_memory_space_constraint(x, pltpu.HBM) for x in held]
         packed = call(
-            pack_kernel, (chips, PACK, 128), [(4 * PACK, 128), (4 * PACK, 128), (4 * 152, 128)],
+            pack_kernel, (chips, PACK, 128), [(4 * PACK + 40, 128), (4 * PACK + 40, 128), (4 * 152 + 48, 128)],
             *held, smem=4,
         )
         planes = lax.all_to_all(packed, "z", 0, 0, tiled=True)
@@ -602,7 +603,7 @@
         zg = both_sides(zp, ("z", "core"), z_pairs)
         back = call(last_kernel, (chips, 40, 128), [state, state], fc, zg, nbt, wet)
         home = lax.all_to_all(back, "z", 0, 0, tiled=True)
-        return call(unpack_kernel, (HELD, 19, 512), [(256, 128)] * 2, home, neighbours)
+        return call(unpack_kernel, (HELD, 19, 512), [(256, 128), (272, 128)], home, neighbours)
 
     placed = (P(axes, None, None), P(axes), P(axes), P(axes), P(axes, None), P(axes, None))
     return jax.shard_map(

time: 74.4 us -> 74.4 us (level)
  no operation moved by 1% of the time
where the time goes in v7:
time: 74.4 us; the launch traced here: 74.2 us
  blocking collectives  65.2 us (88%)
  Pallas kernels  8.89 us (12%)
    all_to_all x1, blocking collectives, shards(): planes = lax.all_to_all(packed, 'z', 0, 0, tiled=True)  23.7 us
    all_gather x3, blocking collectives, both_sides(): y = lax.all_gather(x, names, axis_index_groups=groups)  18.9 us
    all_to_all x1, blocking collectives, shards(): home = lax.all_to_all(back, 'z', 0, 0, tiled=True)  12.5 us
    pallas_call x6, Pallas kernels, call(): pl.pallas_call(kernel, out_shape=shapes if many else shapes[0], in_specs=...  8.89 us
    all_gather x3, blocking collectives, both_sides(): return lax.all_gather(y, 'core')  6.27 us
    all_gather x1, blocking collectives, shards(): got = lax.all_gather(planes, 'core').reshape(group * PACK, 128)  3.87 us

profile of v7, /device:TPU:1, one launch (start us, length us, event | category | flops | bytes accessed | tf_op | source)
XLA Modules:
  0.0 74.2 jit_solution(14552334127078717628)
XLA Ops:
  0.0 1.8 %shard_map.64 = f32[8,88,128]{2,1,0:T(8,128)S(1)} custom-call(s32[3]{0:T(128)} %keep.1, s32[2]{0:T(128)} %send.1, s32[2]{0:T(128)} %dest.1, s32[3,18]{1,0:T(4,128)} %nbr.3, f32[5,19,512]{2,1,0:T(8,128)} %pops.1, s32[3,512]{1,0:T(4,128)} %fluid.1), custom_call_target="tpu_custom_call" | custom-call | tf_op jit(solution)/shard_map/pallas_call | solution.py:548
  1.8 23.7 %all_to_all.10 = f32[8,88,128]{2,1,0:T(8,128)S(1)} all-to-all(f32[8,88,128]{2,1,0:T(8,128)S(1)} %shard_map.64), channel_id=1, replica_groups=mesh['wide'=32,'z'=8,'core'=2] {'z'}, dimensions={0} | all-to-all | bytes 720896 | tf_op jit(solution)/shard_map/all_to_all | solution.py:588
  25.5 3.9 %all-gather = f32[16,88,128]{2,1,0:T(8,128)S(1)} all-gather(f32[8,88,128]{2,1,0:T(8,128)S(1)} %all_to_all.10), channel_id=2, replica_groups=mesh['wide'=32,'z'=8,'core'=2] {'core'}, dimensions={0}, use_global_device_ids=true | all-gather | bytes 1081344 | tf_op jit(solution)/shard_map/all_gather | solution.py:589
  29.3 1.4 %shard_map.65 = (f32[30,32,128]{2,1,0:T(8,128)S(1)}, f32[32,128]{1,0:T(8,128)S(1)}, f32[288,128]{1,0:T(8,128)S(1)}) custom-call(f32[1408,128]{1,0:T(8,128)S(1)} %bitcast.7), custom_call_target="tpu_custom_call" | custom-call | tf_op jit(solution)/shard_map/pallas_call | solution.py:548
  30.8 8.6 %all-gather.1 = f32[576,128]{1,0:T(8,128)S(1)} all-gather(f32[288,128]{1,0:T(8,128)S(1)} %get-tuple-element.16), channel_id=3, replica_groups={{0,16},{2,18},{4,20},{6,22},{8,24},{10,26},{12,28},{14,30},{32,48},{34,..., dimensions={0}, use_global_device_ids=true | all-gather | bytes 442368 | tf_op jit(solution)/shard_map/all_gather | solution.py:577
  39.3 2.2 %all-gather.2 = f32[4,288,128]{2,1,0:T(8,128)S(1)} all-gather(f32[2,288,128]{2,1,0:T(8,128)S(1)} %bitcast.11), channel_id=4, replica_groups=mesh['wide'=32,'z'=8,'core'=2] {'core'}, dimensions={0}, use_global_device_ids=true | all-gather | bytes 884736 | tf_op jit(solution)/shard_map/all_gather | solution.py:578
  41.6 1.7 %shard_map.66 = (f32[19,32,128]{2,1,0:T(8,128)S(1)}, f32[32,128]{1,0:T(8,128)S(1)}, f32[32,128]{1,0:T(8,128)S(1)}, f32[160,128]{1,0:T(8,128)S(1)}) custom-call(f32[30,32,128]{2,1,0:T(8,128)S(1)} %get-tuple-element.14.st, f32[32,128]{1,0:T(8,128)S(1)} %get-tuple-element.15.nb, f32[2,2,288,128]{3,2,1,0:T(8,128)S(1)} %bitcast.8), custom_call_target="tpu_custom_call" | custom-call | tf_op jit(solution)/shard_map/pallas_call | solution.py:548
  43.2 5.2 %all-gather.3 = f32[320,128]{1,0:T(8,128)S(1)} all-gather(f32[160,128]{1,0:T(8,128)S(1)} %get-tuple-element.18), channel_id=5, replica_groups={{0,2},{4,6},{8,10},{12,14},{3,5},{7,9},{11,13},{15,1},{16,18},{20,22},{..., dimensions={0}, use_global_device_ids=true | all-gather | bytes 245760 | tf_op jit(solution)/shard_map/all_gather | solution.py:577
  48.4 2.0 %all-gather.4 = f32[4,160,128]{2,1,0:T(8,128)S(1)} all-gather(f32[2,160,128]{2,1,0:T(8,128)S(1)} %bitcast.12), channel_id=6, replica_groups=mesh['wide'=32,'z'=8,'core'=2] {'core'}, dimensions={0}, use_global_device_ids=true | all-gather | bytes 491520 | tf_op jit(solution)/shard_map/all_gather | solution.py:578
  50.4 1.0 %shard_map.67 = (f32[19,32,128]{2,1,0:T(8,128)S(1)}, f32[160,128]{1,0:T(8,128)S(1)}) custom-call(f32[19,32,128]{2,1,0:T(8,128)S(1)} %get-tuple-element.17.fc, f32[2,2,160,128]{3,2,1,0:T(8,128)S(1)} %bitcast.9, f32[32,128]{1,0:T(8,128)S(1)} %get-tuple-element.19.nbt, f32[32,128]{1,0:T(8,128)S(1)} %get-tuple-element.20.fluid), custom_call_target="tpu_custom_call" | custom-call | tf_op jit(solution)/shard_map/pallas_call | solution.py:548
  51.5 5.2 %all-gather.5 = f32[320,128]{1,0:T(8,128)S(1)} all-gather(f32[160,128]{1,0:T(8,128)S(1)} %get-tuple-element.22), channel_id=7, replica_groups={{0,2},{4,6},{8,10},{12,14},{3,5},{7,9},{11,13},{15,1},{16,18},{20,22},{..., dimensions={0}, use_global_device_ids=true | all-gather | bytes 245760 | tf_op jit(solution)/shard_map/all_gather | solution.py:577
  56.6 2.0 %all-gather.6 = f32[4,160,128]{2,1,0:T(8,128)S(1)} all-gather(f32[2,160,128]{2,1,0:T(8,128)S(1)} %bitcast.13), channel_id=8, replica_groups=mesh['wide'=32,'z'=8,'core'=2] {'core'}, dimensions={0}, use_global_device_ids=true | all-gather | bytes 491520 | tf_op jit(solution)/shard_map/all_gather | solution.py:578
  58.7 1.8 %shard_map.68 = f32[8,40,128]{2,1,0:T(8,128)S(1)} custom-call(f32[19,32,128]{2,1,0:T(8,128)S(1)} %get-tuple-element.21.fc_in, f32[2,2,160,128]{3,2,1,0:T(8,128)S(1)} %bitcast.10, f32[32,128]{1,0:T(8,128)S(1)} %get-tuple-element.19.nbt, f32[32,128]{1,0:T(8,128)S(1)} %get-tuple-element.20.fluid), custom_call_target="tpu_custom_call" | custom-call | tf_op jit(solution)/shard_map/pallas_call | solution.py:548
  60.4 0.0 copy-start
  60.4 12.5 %all_to_all.11.got = f32[8,40,128]{2,1,0:T(8,128)S(1)} all-to-all(f32[8,40,128]{2,1,0:T(8,128)S(1)} %shard_map.68), channel_id=1, replica_groups=mesh['wide'=32,'z'=8,'core'=2] {'z'}, dimensions={0} | all-to-all | bytes 327680 | tf_op jit(solution)/shard_map/all_to_all | solution.py:605
  73.0 0.0 copy-done
  73.0 1.2 %shard_map.69 = f32[3,19,512]{2,1,0:T(8,128)} custom-call(f32[8,40,128]{2,1,0:T(8,128)S(1)} %all_to_all.11.got, s32[3,18]{1,0:T(4,128)S(1)} %copy-done), custom_call_target="tpu_custom_call" | custom-call | tf_op jit(solution)/shard_map/pallas_call | solution.py:548
Async XLA Ops:
  60.4 12.6 %copy-start = (s32[3,18]{1,0:T(4,128)S(1)}, s32[3,18]{1,0:T(4,128)}, u32[]{:S(2)}) copy-start(s32[3,18]{1,0:T(4,128)} %nbr.3) | copy-start | bytes 652

commit v8 on v7

--- a/solution.py
+++ b/solution.py
@@ -294,15 +294,16 @@
     nb[...] = codes
     to_right = ((lax.axis_index("wide") + lax.axis_index("core")) % 2) == 0
     for q in range(8):
-        acc = jnp.zeros((ROWS, 128), F32)
-        for k in range(4):
-            if 4 * q + k >= ARRAYS:
-                continue
-            value = st[4 * q + k]
-            half = jnp.where(to_right, pltpu.roll(value, 64, 1), pltpu.roll(value, 96, 1))
-            half = pltpu.roll(half, 32 * k, 1) if k else half
-            acc = jnp.where(lane // 32 == k, half, acc)
-        xp[ROWS * q : ROWS * q + ROWS, :] = acc
+        halves = []
+        for first in (64, 32):
+            acc = jnp.zeros((ROWS, 128), F32)
+            for k in range(min(4, ARRAYS - 4 * q)):
+                shift = (32 * k - first) % 128
+                value = st[4 * q + k]
+                value = pltpu.roll(value, shift, 1) if shift else value
+                acc = jnp.where(lane // 32 == k, value, acc)
+            halves.append(acc)
+        xp[ROWS * q : ROWS * q + ROWS, :] = jnp.where(to_right, halves[0], halves[1])
     xp[ROWS * 8 : ROWS * 9, :] = codes
 
 

time: 74.4 us -> 74.3 us (level)
  no operation moved by 1% of the time
where the time goes in v8:
time: 74.3 us; the launch traced here: 74 us
  blocking collectives  65.3 us (88%)
  Pallas kernels  8.72 us (12%)
    all_to_all x1, blocking collectives, shards(): planes = lax.all_to_all(packed, 'z', 0, 0, tiled=True)  23.7 us
    all_gather x3, blocking collectives, both_sides(): y = lax.all_gather(x, names, axis_index_groups=groups)  18.9 us
    all_to_all x1, blocking collectives, shards(): home = lax.all_to_all(back, 'z', 0, 0, tiled=True)  12.5 us
    pallas_call x6, Pallas kernels, call(): pl.pallas_call(kernel, out_shape=shapes if many else shapes[0], in_specs=...  8.72 us
    all_gather x3, blocking collectives, both_sides(): return lax.all_gather(y, 'core')  6.27 us
    all_gather x1, blocking collectives, shards(): got = lax.all_gather(planes, 'core').reshape(group * PACK, 128)  3.87 us

profile of v8, /device:TPU:1, one launch (start us, length us, event | category | flops | bytes accessed | tf_op | source)
XLA Modules:
  0.0 74.0 jit_solution(3074951740088575548)
XLA Ops:
  0.0 1.8 %shard_map.64 = f32[8,88,128]{2,1,0:T(8,128)S(1)} custom-call(s32[3]{0:T(128)} %keep.1, s32[2]{0:T(128)} %send.1, s32[2]{0:T(128)} %dest.1, s32[3,18]{1,0:T(4,128)} %nbr.3, f32[5,19,512]{2,1,0:T(8,128)} %pops.1, s32[3,512]{1,0:T(4,128)} %fluid.1), custom_call_target="tpu_custom_call" | custom-call | tf_op jit(solution)/shard_map/pallas_call | solution.py:549
  1.8 23.7 %all_to_all.10 = f32[8,88,128]{2,1,0:T(8,128)S(1)} all-to-all(f32[8,88,128]{2,1,0:T(8,128)S(1)} %shard_map.64), channel_id=1, replica_groups=mesh['wide'=32,'z'=8,'core'=2] {'z'}, dimensions={0} | all-to-all | bytes 720896 | tf_op jit(solution)/shard_map/all_to_all | solution.py:589
  25.5 3.9 %all-gather = f32[16,88,128]{2,1,0:T(8,128)S(1)} all-gather(f32[8,88,128]{2,1,0:T(8,128)S(1)} %all_to_all.10), channel_id=2, replica_groups=mesh['wide'=32,'z'=8,'core'=2] {'core'}, dimensions={0}, use_global_device_ids=true | all-gather | bytes 1081344 | tf_op jit(solution)/shard_map/all_gather | solution.py:590
  29.3 1.3 %shard_map.65 = (f32[30,32,128]{2,1,0:T(8,128)S(1)}, f32[32,128]{1,0:T(8,128)S(1)}, f32[288,128]{1,0:T(8,128)S(1)}) custom-call(f32[1408,128]{1,0:T(8,128)S(1)} %bitcast.7), custom_call_target="tpu_custom_call" | custom-call | tf_op jit(solution)/shard_map/pallas_call | solution.py:549
  30.6 8.6 %all-gather.1 = f32[576,128]{1,0:T(8,128)S(1)} all-gather(f32[288,128]{1,0:T(8,128)S(1)} %get-tuple-element.16), channel_id=3, replica_groups={{0,16},{2,18},{4,20},{6,22},{8,24},{10,26},{12,28},{14,30},{32,48},{34,..., dimensions={0}, use_global_device_ids=true | all-gather | bytes 442368 | tf_op jit(solution)/shard_map/all_gather | solution.py:578
  39.2 2.2 %all-gather.2 = f32[4,288,128]{2,1,0:T(8,128)S(1)} all-gather(f32[2,288,128]{2,1,0:T(8,128)S(1)} %bitcast.11), channel_id=4, replica_groups=mesh['wide'=32,'z'=8,'core'=2] {'core'}, dimensions={0}, use_global_device_ids=true | all-gather | bytes 884736 | tf_op jit(solution)/shard_map/all_gather | solution.py:579
  41.4 1.7 %shard_map.66 = (f32[19,32,128]{2,1,0:T(8,128)S(1)}, f32[32,128]{1,0:T(8,128)S(1)}, f32[32,128]{1,0:T(8,128)S(1)}, f32[160,128]{1,0:T(8,128)S(1)}) custom-call(f32[30,32,128]{2,1,0:T(8,128)S(1)} %get-tuple-element.14.st, f32[32,128]{1,0:T(8,128)S(1)} %get-tuple-element.15.nb, f32[2,2,288,128]{3,2,1,0:T(8,128)S(1)} %bitcast.8), custom_call_target="tpu_custom_call" | custom-call | tf_op jit(solution)/shard_map/pallas_call | solution.py:549
  43.1 5.2 %all-gather.3 = f32[320,128]{1,0:T(8,128)S(1)} all-gather(f32[160,128]{1,0:T(8,128)S(1)} %get-tuple-element.18), channel_id=5, replica_groups={{0,2},{4,6},{8,10},{12,14},{3,5},{7,9},{11,13},{15,1},{16,18},{20,22},{..., dimensions={0}, use_global_device_ids=true | all-gather | bytes 245760 | tf_op jit(solution)/shard_map/all_gather | solution.py:578
  48.2 2.0 %all-gather.4 = f32[4,160,128]{2,1,0:T(8,128)S(1)} all-gather(f32[2,160,128]{2,1,0:T(8,128)S(1)} %bitcast.12), channel_id=6, replica_groups=mesh['wide'=32,'z'=8,'core'=2] {'core'}, dimensions={0}, use_global_device_ids=true | all-gather | bytes 491520 | tf_op jit(solution)/shard_map/all_gather | solution.py:579
  50.3 1.0 %shard_map.67 = (f32[19,32,128]{2,1,0:T(8,128)S(1)}, f32[160,128]{1,0:T(8,128)S(1)}) custom-call(f32[19,32,128]{2,1,0:T(8,128)S(1)} %get-tuple-element.17.fc, f32[2,2,160,128]{3,2,1,0:T(8,128)S(1)} %bitcast.9, f32[32,128]{1,0:T(8,128)S(1)} %get-tuple-element.19.nbt, f32[32,128]{1,0:T(8,128)S(1)} %get-tuple-element.20.fluid), custom_call_target="tpu_custom_call" | custom-call | tf_op jit(solution)/shard_map/pallas_call | solution.py:549
  51.3 5.2 %all-gather.5 = f32[320,128]{1,0:T(8,128)S(1)} all-gather(f32[160,128]{1,0:T(8,128)S(1)} %get-tuple-element.22), channel_id=7, replica_groups={{0,2},{4,6},{8,10},{12,14},{3,5},{7,9},{11,13},{15,1},{16,18},{20,22},{..., dimensions={0}, use_global_device_ids=true | all-gather | bytes 245760 | tf_op jit(solution)/shard_map/all_gather | solution.py:578
  56.5 2.0 %all-gather.6 = f32[4,160,128]{2,1,0:T(8,128)S(1)} all-gather(f32[2,160,128]{2,1,0:T(8,128)S(1)} %bitcast.13), channel_id=8, replica_groups=mesh['wide'=32,'z'=8,'core'=2] {'core'}, dimensions={0}, use_global_device_ids=true | all-gather | bytes 491520 | tf_op jit(solution)/shard_map/all_gather | solution.py:579
  58.5 1.8 %shard_map.68 = f32[8,40,128]{2,1,0:T(8,128)S(1)} custom-call(f32[19,32,128]{2,1,0:T(8,128)S(1)} %get-tuple-element.21.fc_in, f32[2,2,160,128]{3,2,1,0:T(8,128)S(1)} %bitcast.10, f32[32,128]{1,0:T(8,128)S(1)} %get-tuple-element.19.nbt, f32[32,128]{1,0:T(8,128)S(1)} %get-tuple-element.20.fluid), custom_call_target="tpu_custom_call" | custom-call | tf_op jit(solution)/shard_map/pallas_call | solution.py:549
  60.3 0.0 copy-start
  60.3 12.5 %all_to_all.11.got = f32[8,40,128]{2,1,0:T(8,128)S(1)} all-to-all(f32[8,40,128]{2,1,0:T(8,128)S(1)} %shard_map.68), channel_id=1, replica_groups=mesh['wide'=32,'z'=8,'core'=2] {'z'}, dimensions={0} | all-to-all | bytes 327680 | tf_op jit(solution)/shard_map/all_to_all | solution.py:606
  72.8 0.0 copy-done
  72.8 1.2 %shard_map.69 = f32[3,19,512]{2,1,0:T(8,128)} custom-call(f32[8,40,128]{2,1,0:T(8,128)S(1)} %all_to_all.11.got, s32[3,18]{1,0:T(4,128)S(1)} %copy-done), custom_call_target="tpu_custom_call" | custom-call | tf_op jit(solution)/shard_map/pallas_call | solution.py:549
Async XLA Ops:
  60.3 12.6 %copy-start = (s32[3,18]{1,0:T(4,128)S(1)}, s32[3,18]{1,0:T(4,128)}, u32[]{:S(2)}) copy-start(s32[3,18]{1,0:T(4,128)} %nbr.3) | copy-start | bytes 652
